TPU v7x, 32 devices: a whole 2x2x4 slice. The times are simulated.
32 devices in a mesh: fsdp: 4 (over z), ctx: 4 (over x, core), tp: 2 (over y).
Axes of the slice: x: 2, y: 2, z: 4, core: 2. Of those that a mesh axis runs over, the one named last changes fastest.
Arguments:
- layer_input: bfloat16 [8192, 1024], P(('fsdp', 'ctx')), may hold values from -6 to 6
- cotangent: bfloat16 [8192, 1024], P(('fsdp', 'ctx')), may hold values from -6 to 6
- dealing: int32 [4, 2048], P('fsdp'), may hold values from 0 to 2047, each once within a row
- segments: int32 [4, 2048], P('fsdp'), may hold values from 0 to 2, never falling along the last dimension, each value on 1 to 1024 neighbouring positions
- lengths: int32 [4, 3], P('fsdp'), may hold values from 256 to 1024
- routes: int32 [8192, 8], P(('fsdp', 'ctx')), may hold values from 0 to 31, all different within a row; in each aligned block of 512 rows (0 to 511, 512 to 1023, ...) at most 192 rows name the same one
- attention_gain: bfloat16 [1024], P('fsdp'), may hold values from 0.5 to 1.5
- query_weight: bfloat16 [1024, 1024], P('fsdp', 'tp'), may hold values from -0.1875 to 0.1875
- key_projection: bfloat16 [1024, 512], P('fsdp', 'tp'), may hold values from -0.1875 to 0.1875
- value_projection: bfloat16 [1024, 512], P('fsdp', 'tp'), may hold values from -0.1875 to 0.1875
- output_weight: bfloat16 [1024, 1024], P('tp', 'fsdp'), may hold values from -2 to 2
- mixture_gain: bfloat16 [1024], P('fsdp'), may hold values from 0.5 to 1.5
- router_weight: bfloat16 [1024, 32], P('fsdp'), may hold values from -0.09375 to 0.09375
- gate_weight: bfloat16 [32, 1024, 512], P('fsdp', None, 'tp'), may hold values from -0.1875 to 0.1875
- up_weight: bfloat16 [32, 1024, 512], P('fsdp', None, 'tp'), may hold values from -0.1875 to 0.1875
- down_weight: bfloat16 [32, 512, 1024], P('fsdp', 'tp'), may hold values from -1 to 1
Outputs:
- layer_output: bfloat16 [8192, 1024], P(('fsdp', 'ctx'))
- grad_input: float32 [8192, 1024], P(('fsdp', 'ctx'))
- grad_attention_gain: float32 [1024], P('fsdp')
- grad_query_weight: float32 [1024, 1024], P('fsdp', 'tp')
- grad_key_weight: float32 [1024, 512], P('fsdp', 'tp')
- grad_value_weight: float32 [1024, 512], P('fsdp', 'tp')
- grad_output_weight: float32 [1024, 1024], P('tp', 'fsdp')
- grad_mixture_gain: float32 [1024], P('fsdp')
- grad_router_weight: float32 [1024, 32], P('fsdp')
- grad_gate_weight: float32 [32, 1024, 512], P('fsdp', None, 'tp')
- grad_up_weight: float32 [32, 1024, 512], P('fsdp', None, 'tp')
- grad_down_weight: float32 [32, 512, 1024], P('fsdp', 'tp')
Inputs may be any that keep to these rules, and one draw needn't show every extreme that they name: `dealing`: each row is a permutation of the places 0 to 2047. Along a row the segment numbers never fall; each of the 3 segments holds 1 to 1024 places, one exactly 1024. `lengths`: A segment's first min(length, its size) positions are live, the rest are pads. `routes`: each row names 8 different experts; among the 512 rows of one device no expert is named more than 192 times, a bound that some block reaches.
All inputs are finite; a program needn't handle non-finite values.
Results may differ from a plain program's by a relative error of at most 0.015.
Values may be sent and summed in bfloat16 or wider, within the bound.
No kernel may reach another device: no remote copies, remote signals or barrier semaphores. Data moves between devices by JAX's collectives and lax.ppermute only.
A program may use at most 256 MiB of HBM per device.

v0:
```python
import jax
import jax.numpy as jnp
from jax import lax
from jax.experimental import pallas as pl
from jax.experimental.pallas import tpu as pltpu
from jax.sharding import PartitionSpec as P


HEAD_SIZE = 64
ROW_TILE = 512

epsilon = 1e-06
rope_base = 10000.0


f32 = jnp.float32
bf16 = jnp.bfloat16


def shift(size, k):
    return [(i, (i + k) % size) for i in range(size)]


def flip(size, bit):
    return [(i, i ^ bit) for i in range(size)]


def swap_tp(x):
    return lax.ppermute(x, "tp", flip(lax.axis_size("tp"), 1))


def swap_core(x):
    return lax.ppermute(x, "ctx", flip(lax.axis_size("ctx"), 1))


def swap_far(x):
    return lax.ppermute(x, "ctx", flip(lax.axis_size("ctx"), 2))


def shift_fsdp(x, k):
    return lax.ppermute(x, "fsdp", shift(lax.axis_size("fsdp"), k))


def few_groups():
    return lax.axis_size("fsdp") <= 8


def pick(x, index, axis=0):
    return lax.dynamic_index_in_dim(x, index, axis, keepdims=False)


def reduce_small(sums):
    groups = lax.axis_size("fsdp")
    here = lax.axis_index("fsdp")
    shard = sums.shape[1] // groups
    sums = sums + swap_tp(sums)
    sums = sums + swap_core(sums)
    sums = sums + swap_far(sums)
    if not few_groups():
        return lax.psum_scatter(sums, "fsdp", scatter_dimension=1, tiled=True)

    def block(k):
        return lax.dynamic_slice_in_dim(sums, ((here + k) % groups) * shard, shard, 1)

    total = block(0)
    for k in range(1, groups):
        total = total + shift_fsdp(block(k), k)
    return total


def put_pair(index, mine, other, axis=0):
    first = index == 0
    return jnp.concatenate(
        [jnp.where(first, mine, other), jnp.where(first, other, mine)], axis
    )


def gather_rows(weight):
    size = lax.axis_size("fsdp")
    if not few_groups():
        return lax.all_gather(weight, "fsdp", axis=0, tiled=True)
    here = lax.axis_index("fsdp")
    parity = lax.axis_index("ctx") % 2
    rows, cols = weight.shape
    half = lax.dynamic_slice_in_dim(weight, parity * (rows // 2), rows // 2, 0)
    full = jnp.zeros((size * rows, cols), weight.dtype)
    full = lax.dynamic_update_slice(full, weight, (here * rows, 0))
    for k in range(1, size):
        mine = shift_fsdp(half, k)
        other = swap_core(mine)
        base = ((here + size - k) % size) * rows
        full = lax.dynamic_update_slice(full, mine, (base + parity * (rows // 2), 0))
        full = lax.dynamic_update_slice(full, other, (base + (1 - parity) * (rows // 2), 0))
    return full


def gather_small(x):
    size = lax.axis_size("fsdp")
    if not few_groups():
        return lax.all_gather(x, "fsdp", axis=0)
    here = lax.axis_index("fsdp")
    full = jnp.zeros((size,) + x.shape, x.dtype)
    zeros = (0,) * x.ndim
    for k in range(size):
        part = x if k == 0 else shift_fsdp(x, k)
        full = lax.dynamic_update_slice(full, part[None], ((here + size - k) % size,) + zeros)
    return full


def reduce_blocks(blocks):
    size = lax.axis_size("fsdp")
    here = lax.axis_index("fsdp")
    parity = lax.axis_index("ctx") % 2
    rows = blocks.shape[1]
    if not few_groups():
        own = lax.psum_scatter(blocks, "fsdp", scatter_dimension=0, tiled=True)[0]
        return lax.psum(own, "ctx")
    halves = blocks.reshape(size, 2, rows // 2, blocks.shape[2])
    came = swap_core(pick(halves, 1 - parity, 1).astype(bf16))
    mine = pick(halves, parity, 1) + came.astype(f32)
    total = pick(mine, here)
    for k in range(1, size):
        total = total + shift_fsdp(pick(mine, (here + k) % size).astype(bf16), k).astype(f32)
    low = lax.reduce_precision(total, 8, 7)
    total = low + swap_far(low.astype(bf16)).astype(f32)
    return put_pair(parity, total, swap_core(total))


def rope_tables(places, starts):
    half = HEAD_SIZE // 2
    freqs = rope_base ** (-(jnp.arange(half, dtype=f32) * (2.0 / HEAD_SIZE)))
    angles = (places - starts).astype(f32)[:, None] * freqs[None, :]
    cosine, sine = jnp.cos(angles), jnp.sin(angles)
    return (
        jnp.concatenate([cosine] * 4, 1),
        jnp.concatenate([-sine, sine, -sine, sine], 1),
    )


def rotate(x, cosine, sine, direction):
    lane = lax.broadcasted_iota(jnp.int32, x.shape, 1)
    first = lane % HEAD_SIZE < HEAD_SIZE // 2
    partner = jnp.where(first, pltpu.roll(x, 128 - HEAD_SIZE // 2, 1), pltpu.roll(x, HEAD_SIZE // 2, 1))
    return x * cosine + (partner * sine) * direction


def contract_rows(left, right):
    return lax.dot_general(left, right, (((0,), (0,)), ((), ())), preferred_element_type=f32)


def contract_cols(left, right):
    return lax.dot_general(left, right, (((1,), (1,)), ((), ())), preferred_element_type=f32)


def chosen_softmax(logits, mark):
    chosen = mark > 0.5
    top = jnp.max(jnp.where(chosen, logits, -3e38), -1, keepdims=True)
    powers = jnp.where(chosen, jnp.exp(logits - top), 0.0)
    return powers / jnp.sum(powers, -1, keepdims=True)


def expert_kernel(
    base_ref,
    x_mine,
    x_other,
    g_mine,
    g_other,
    mark,
    router,
    gate_w,
    up_w,
    down_w,
    dx_mine,
    dx_other,
    hidden_out,
    dgate_out,
    dup_out,
    score_out,
    x_all,
    g_all,
    gate_cols,
    total,
):
    step = pl.program_id(1)
    last = pl.num_programs(1) - 1
    half = x_mine.shape[0]

    @pl.when(step == 0)
    def _():
        x_all[:half] = x_mine[...]
        x_all[half:] = x_other[...]
        g_all[:half] = g_mine[...]
        g_all[half:] = g_other[...]
        logits = jnp.dot(x_all[...], router[...], preferred_element_type=f32)
        marks = mark[...].astype(f32)
        gate_cols[...] = jnp.where(marks > 1.5, chosen_softmax(logits, marks), 0.0)
        total[...] = jnp.zeros_like(total)
        score_out[...] = jnp.zeros_like(score_out)

    for at in range(0, 2 * half, half):
        rows = slice(at, at + half)
        x = x_all[rows]
        gate_act = jnp.dot(x, gate_w[0], preferred_element_type=f32)
        up_act = jnp.dot(x, up_w[0], preferred_element_type=f32)
        raw = contract_cols(g_all[rows], down_w[0])
        columns = gate_cols[rows]
        lane = lax.broadcasted_iota(jnp.int32, columns.shape, 1)
        weight = jnp.sum(jnp.where(lane == base_ref[0] + step, columns, 0.0), 1, keepdims=True)
        sigmoid = jax.nn.sigmoid(gate_act)
        silu = gate_act * sigmoid
        hidden = silu * up_act
        dot_col = jnp.sum(hidden * raw, 1, keepdims=True)
        scores = score_out[rows]
        place = lax.broadcasted_iota(jnp.int32, scores.shape, 1)
        score_out[rows] = jnp.where(place == step, dot_col, scores)
        hidden_out[rows] = (hidden * weight).astype(bf16)
        grad_hidden = raw * weight
        dgate = (grad_hidden * up_act * (sigmoid * (1.0 + gate_act * (1.0 - sigmoid)))).astype(bf16)
        dup = (grad_hidden * silu).astype(bf16)
        dgate_out[rows] = dgate
        dup_out[rows] = dup
        total[rows] += contract_cols(dgate, gate_w[0]) + contract_cols(dup, up_w[0])

    @pl.when(step == last)
    def _():
        dx_mine[...] = total[:half].astype(bf16)
        dx_other[...] = total[half:].astype(bf16)


def run_experts(base, x_mine, x_other, grads, mark, router, gate_w, up_w, down_w):
    rows, width = x_mine.shape
    half = min(rows, ROW_TILE // 2)
    tiles = rows // half
    experts, _, hidden = gate_w.shape
    columns = router.shape[1]
    tile_rows = 2 * half
    part = pl.BlockSpec((half, width), lambda i, l, b: (i, 0))
    wide = pl.BlockSpec((tile_rows, hidden), lambda i, l, b: (i, l))
    flops = 2 * tiles * experts * tile_rows * width * hidden * 5
    return pl.pallas_call(
        expert_kernel,
        out_shape=(
            jax.ShapeDtypeStruct((rows, width), bf16),
            jax.ShapeDtypeStruct((rows, width), bf16),
            jax.ShapeDtypeStruct((2 * rows, experts * hidden), bf16),
            jax.ShapeDtypeStruct((2 * rows, experts * hidden), bf16),
            jax.ShapeDtypeStruct((2 * rows, experts * hidden), bf16),
            jax.ShapeDtypeStruct((2 * rows, experts), f32),
        ),
        grid_spec=pltpu.PrefetchScalarGridSpec(
            num_scalar_prefetch=1,
            grid=(tiles, experts),
            in_specs=[
                part,
                part,
                pl.BlockSpec((half, width), lambda i, l, b: (b[1] + 2 * i, 0)),
                pl.BlockSpec((half, width), lambda i, l, b: (b[2] + 2 * i, 0)),
                pl.BlockSpec((tile_rows, columns), lambda i, l, b: (i, 0)),
                pl.BlockSpec((width, columns), lambda i, l, b: (0, 0)),
                pl.BlockSpec((1, width, hidden), lambda i, l, b: (l, 0, 0)),
                pl.BlockSpec((1, width, hidden), lambda i, l, b: (l, 0, 0)),
                pl.BlockSpec((1, hidden, width), lambda i, l, b: (l, 0, 0)),
            ],
            out_specs=[
                part,
                part,
                wide,
                wide,
                wide,
                pl.BlockSpec((tile_rows, experts), lambda i, l, b: (i, 0)),
            ],
            scratch_shapes=[
                pltpu.VMEM((tile_rows, width), bf16),
                pltpu.VMEM((tile_rows, width), bf16),
                pltpu.VMEM((tile_rows, columns), f32),
                pltpu.VMEM((tile_rows, width), f32),
            ],
        ),
        cost_estimate=pl.CostEstimate(
            flops=flops,
            bytes_accessed=tiles * 3 * experts * hidden * width * 2 + rows * width * 16,
            transcendentals=tiles * tile_rows * experts * hidden,
        ),
        compiler_params=pltpu.CompilerParams(
            dimension_semantics=("arbitrary", "arbitrary"), vmem_limit_bytes=56 * 2**20
        ),
        name="experts",
    )(base, x_mine, x_other, grads, grads, mark, router, gate_w, up_w, down_w)


def weight_grads(picks, part, stride, row_arrays, acts_list, come, rows_first, hidden):
    chunks = len(row_arrays) // 2
    results = len(acts_list)
    width = row_arrays[0].shape[1]
    tile = min(part, 256)
    tiles = part // tile
    experts = acts_list[0][0].shape[1] // hidden
    wide = width // 2
    shape = (wide, hidden) if rows_first else (hidden, wide)

    def kernel(*refs):
        refs = refs[1:]
        row_refs = refs[: 2 * chunks]
        refs = refs[2 * chunks :]
        act_refs = refs[: results * chunks]
        refs = refs[results * chunks :]
        come_refs = refs[: len(come)]
        refs = refs[len(come) :]
        out_refs = refs[:results]
        sums = refs[results : 2 * results]
        turned = refs[2 * results]
        expert, step = pl.program_id(0), pl.program_id(1)

        def fill():
            for i in range(chunks):
                for h in range(2):
                    block = row_refs[2 * i + h][...]
                    at = (2 * i + h) * tile
                    if rows_first:
                        turned[:, at : at + tile] = block.T
                    else:
                        turned[at : at + tile, :] = block

        if tiles == 1:
            pl.when(expert == 0)(fill)
        else:
            fill()
        for r in range(results):
            value = None
            for i in range(chunks):
                acts = act_refs[r * chunks + i][...]
                at = slice(2 * i * tile, 2 * (i + 1) * tile)
                if rows_first:
                    term = jnp.dot(turned[:, at], acts, preferred_element_type=f32)
                else:
                    term = contract_rows(acts, turned[at])
                value = term if value is None else value + term
            if tiles > 1:
                value = value + jnp.where(step == 0, 0.0, sums[r][...])
                sums[r][...] = value
            if come:
                value = value + come_refs[r][0].astype(f32)
            out_refs[r][0] = value.astype(bf16)

    def row_spec(n):
        return pl.BlockSpec((tile, wide), lambda e, i, h: (h[1 + n] + stride * i, h[0]))

    act_spec = pl.BlockSpec((2 * tile, hidden), lambda e, i, h: (i, e))
    out_spec = pl.BlockSpec((1,) + shape, lambda e, i, h: (e, 0, 0))
    turned_shape = (wide, 2 * chunks * tile) if rows_first else (2 * chunks * tile, wide)
    return pl.pallas_call(
        kernel,
        out_shape=tuple(jax.ShapeDtypeStruct((experts,) + shape, bf16) for _ in range(results)),
        grid_spec=pltpu.PrefetchScalarGridSpec(
            num_scalar_prefetch=1,
            grid=(experts, tiles),
            in_specs=[row_spec(n) for n in range(2 * chunks)]
            + [act_spec] * (results * chunks)
            + [out_spec] * len(come),
            out_specs=[out_spec] * results,
            scratch_shapes=[pltpu.VMEM(shape, f32) for _ in range(results)]
            + [pltpu.VMEM(turned_shape, bf16)],
        ),
        cost_estimate=pl.CostEstimate(
            flops=2 * results * chunks * 2 * part * experts * hidden * wide,
            bytes_accessed=results * chunks * 2 * part * experts * hidden * 2
            + chunks * 2 * part * wide * 2
            + results * experts * hidden * wide * 4,
            transcendentals=0,
        ),
        compiler_params=pltpu.CompilerParams(
            dimension_semantics=("arbitrary", "arbitrary"), vmem_limit_bytes=56 * 2**20
        ),
    )(
        picks,
        *row_arrays,
        *[a for acts in acts_list for a in acts],
        *come,
    )


def join_halves(parity, mine, other, axis):
    experts, rows, cols = mine.shape
    step = 2 if experts % 2 == 0 else 1
    shape = (2 * rows, cols) if axis == 1 else (rows, 2 * cols)

    def kernel(parity_ref, mine_ref, other_ref, out):
        extent = rows if axis == 1 else cols
        for which, ref in ((parity_ref[0], mine_ref), (1 - parity_ref[0], other_ref)):
            at = pl.ds(pl.multiple_of(which * extent, extent), extent)
            if axis == 1:
                out[:, at, :] = ref[...].astype(f32)
            else:
                out[:, :, at] = ref[...].astype(f32)

    spec = pl.BlockSpec((step, rows, cols), lambda e, p: (e, 0, 0))
    return pl.pallas_call(
        kernel,
        out_shape=jax.ShapeDtypeStruct((experts,) + shape, f32),
        grid_spec=pltpu.PrefetchScalarGridSpec(
            num_scalar_prefetch=1,
            grid=(experts // step,),
            in_specs=[spec, spec],
            out_specs=pl.BlockSpec((step,) + shape, lambda e, p: (e, 0, 0)),
        ),
        cost_estimate=pl.CostEstimate(
            flops=0, bytes_accessed=experts * rows * cols * 12, transcendentals=0
        ),
        name="join",
    )(parity, mine, other)


def project(normed, weight, cosine, sine, rope_cols, factor):
    rows = normed.shape[0]
    cols = weight.shape[1]

    def kernel(x, w, c, s, out):
        value = jnp.dot(x[...], w[...], preferred_element_type=f32)
        for at in range(0, cols, 128):
            part = value[:, at : at + 128]
            if at < rope_cols:
                part = rotate(part, c[...], s[...], 1.0)
            out[:, at : at + 128] = (part * factor).astype(bf16)

    return pl.pallas_call(
        kernel,
        out_shape=jax.ShapeDtypeStruct((rows, cols), bf16),
        cost_estimate=pl.CostEstimate(
            flops=2 * rows * cols * normed.shape[1], bytes_accessed=4 * 2**20, transcendentals=0
        ),
        name="project",
    )(normed, weight, cosine, sine)


def keys_back(kept, near, far, cosine, sine):
    rows, cols = far.shape

    def kernel(a, b, d, c, s, out):
        value = a[0].astype(f32) + b[0].astype(f32) + d[...].astype(f32)
        for at in range(0, cols, 128):
            part = value[:, at : at + 128]
            if at < cols // 2:
                part = rotate(part, c[...], s[...], -1.0)
            out[:, at : at + 128] = part.astype(bf16)

    one = pl.BlockSpec((1, rows, cols), lambda i: (0, 0, 0))
    full = pl.BlockSpec((rows, cols), lambda i: (0, 0))
    table = pl.BlockSpec((rows, 128), lambda i: (0, 0))
    return pl.pallas_call(
        kernel,
        out_shape=jax.ShapeDtypeStruct((rows, cols), bf16),
        grid=(1,),
        in_specs=[one, one, full, table, table],
        out_specs=full,
        cost_estimate=pl.CostEstimate(flops=2**20, bytes_accessed=3 * 2**20, transcendentals=0),
        name="keys_back",
    )(kept, near, far, cosine, sine)


def fill_blocks(pieces, keep, tile):
    for source in range(len(pieces)):
        for j in range(keep.shape[0]):
            keep[j, source * tile : (source + 1) * tile, :] = pieces[source][
                j * tile : (j + 1) * tile, :
            ]


def attend(bounds, query, pieces, query_info, key_places, kv_heads):
    rows, width = query.shape
    kv_cols = pieces[0].shape[1]
    group = width // HEAD_SIZE // kv_heads
    peers = len(pieces)
    tile = rows // 4
    span = peers * tile

    def kernel(bounds_ref, q, *refs):
        piece_refs = refs[:peers]
        info, places, out, totals, keep, peaks, sums, accs = refs[peers:]
        i = pl.program_id(0)
        pl.when(i == 0)(lambda: fill_blocks(piece_refs, keep, tile))
        high = jnp.concatenate([info[:, 0:1]] * group, 0)
        low = jnp.concatenate([info[:, 1:2]] * group, 0)
        first, stop = bounds_ref[i], bounds_ref[4 + i]
        lane = lax.broadcasted_iota(jnp.int32, totals.shape, 1)
        peaks[...] = jnp.full(peaks.shape, -1e30, f32)
        sums[...] = jnp.zeros_like(sums)
        accs[...] = jnp.zeros_like(accs)

        def step(j, carry):
            row = places[j]
            allowed = (row <= high) & (row >= low)
            for head in range(kv_heads):
                at = head * group * HEAD_SIZE
                q_head = jnp.concatenate(
                    [q[:, at + g * HEAD_SIZE : at + (g + 1) * HEAD_SIZE] for g in range(group)], 0
                )
                keys = keep[j, :, head * HEAD_SIZE : (head + 1) * HEAD_SIZE]
                first_val = kv_cols // 2 + head * HEAD_SIZE
                vals = keep[j, :, first_val : first_val + HEAD_SIZE]
                scores = jnp.where(allowed, contract_cols(q_head, keys), -1e30)
                peak = peaks[head]
                new_peak = jnp.maximum(peak, jnp.max(scores, 1, keepdims=True))
                shrink = jnp.exp(peak - new_peak)
                powers = jnp.exp(scores - new_peak)
                peaks[head] = new_peak
                sums[head] = sums[head] * shrink + jnp.sum(powers, 1, keepdims=True)
                accs[head] = accs[head] * shrink + jnp.dot(
                    powers.astype(bf16), vals, preferred_element_type=f32
                )
            return carry

        lax.fori_loop(first, stop, step, 0)
        collected = jnp.zeros(totals.shape, f32)
        for head in range(kv_heads):
            at = head * group * HEAD_SIZE
            total = sums[head]
            acc = (accs[head] / total).astype(bf16)
            logs = peaks[head] + jnp.log(total)
            for g in range(group):
                out[:, at + g * HEAD_SIZE : at + (g + 1) * HEAD_SIZE] = acc[g * tile : (g + 1) * tile]
                collected = jnp.where(
                    lane == head * group + g, logs[g * tile : (g + 1) * tile], collected
                )
        totals[...] = collected

    full = pl.BlockSpec((rows, kv_cols), lambda i, b: (0, 0))
    heads = width // HEAD_SIZE
    return pl.pallas_call(
        kernel,
        out_shape=(
            jax.ShapeDtypeStruct((rows, width), bf16),
            jax.ShapeDtypeStruct((rows, heads), f32),
        ),
        grid_spec=pltpu.PrefetchScalarGridSpec(
            num_scalar_prefetch=1,
            grid=(4,),
            in_specs=[pl.BlockSpec((tile, width), lambda i, b: (i, 0))]
            + [full] * peers
            + [
                pl.BlockSpec((tile, 2), lambda i, b: (i, 0)),
                pl.BlockSpec((4, 1, span), lambda i, b: (0, 0, 0)),
            ],
            out_specs=[
                pl.BlockSpec((tile, width), lambda i, b: (i, 0)),
                pl.BlockSpec((tile, heads), lambda i, b: (i, 0)),
            ],
            scratch_shapes=[
                pltpu.VMEM((4, span, kv_cols), bf16),
                pltpu.VMEM((kv_heads, group * tile, 1), f32),
                pltpu.VMEM((kv_heads, group * tile, 1), f32),
                pltpu.VMEM((kv_heads, group * tile, HEAD_SIZE), f32),
            ],
        ),
        cost_estimate=pl.CostEstimate(
            flops=4 * rows * rows * peers * width, bytes_accessed=4 * 2**20, transcendentals=2**22
        ),
        name="attend",
    )(bounds, query, *pieces, query_info, key_places)


def attend_back(bounds, query, grads, pieces, logs, inner, query_rows, key_cols, cosine, sine, kv_heads, scale):
    rows, width = query.shape
    kv_cols = pieces[0].shape[1]
    heads = width // HEAD_SIZE
    group = heads // kv_heads
    peers = len(pieces)
    tile = rows // 4
    span = peers * tile

    def kernel(bounds_ref, q, go, *refs):
        piece_refs = refs[:peers]
        log_ref, inner_ref, info, places, cos_ref, sin_ref = refs[peers : peers + 6]
        dq_out, kept, sent, keep, dk, dv, turned = refs[peers + 6 :]
        i = pl.program_id(0)

        @pl.when(i == 0)
        def _():
            fill_blocks(piece_refs, keep, tile)
            dk[...] = jnp.zeros_like(dk)
            dv[...] = jnp.zeros_like(dv)

        high = jnp.concatenate([info[0:1, :]] * group, 1)
        low = jnp.concatenate([info[1:2, :]] * group, 1)
        first, stop = bounds_ref[i], bounds_ref[4 + i]
        turned[...] = jnp.zeros_like(turned)

        def step(j, carry):
            column = places[j]
            allowed = (column <= high) & (column >= low)
            for head in range(kv_heads):
                at = head * group * HEAD_SIZE

                def stacked(ref):
                    return jnp.concatenate(
                        [ref[:, at + g * HEAD_SIZE : at + (g + 1) * HEAD_SIZE] for g in range(group)],
                        0,
                    )

                def side_by_side(ref):
                    return jnp.concatenate(
                        [ref[head * group + g : head * group + g + 1, :] for g in range(group)], 1
                    )

                q_head, go_head = stacked(q), stacked(go)
                keys = keep[j, :, head * HEAD_SIZE : (head + 1) * HEAD_SIZE]
                first_val = kv_cols // 2 + head * HEAD_SIZE
                vals = keep[j, :, first_val : first_val + HEAD_SIZE]
                scores = contract_cols(keys, q_head)
                probs = jnp.where(allowed, jnp.exp(scores - side_by_side(log_ref)), 0.0)
                grad_probs = contract_cols(vals, go_head)
                grad_scores = (probs * (grad_probs - side_by_side(inner_ref))).astype(bf16)
                dv[head, j] += jnp.dot(probs.astype(bf16), go_head, preferred_element_type=f32)
                dk[head, j] += jnp.dot(grad_scores, q_head, preferred_element_type=f32)
                turned[head] += contract_rows(keys, grad_scores)
            return carry

        lax.fori_loop(first, stop, step, 0)
        for head in range(kv_heads):
            at = head * group * HEAD_SIZE
            dq = turned[head].T
            dq = jnp.concatenate([dq[g * tile : (g + 1) * tile] for g in range(group)], 1) * scale
            dq_out[:, at : at + group * HEAD_SIZE] = rotate(
                dq, cos_ref[...], sin_ref[...], -1.0
            ).astype(bf16)

        @pl.when(i == pl.num_programs(0) - 1)
        def _():
            for source in range(peers):
                target = sent if source % 2 else kept
                for j in range(4):
                    for part, acc in enumerate((dk, dv)):
                        block = jnp.concatenate(
                            [acc[h, j, source * tile : (source + 1) * tile, :] for h in range(kv_heads)], 1
                        )
                        target[
                            source // 2,
                            j * tile : (j + 1) * tile,
                            part * kv_cols // 2 : (part + 1) * kv_cols // 2,
                        ] = block.astype(bf16)

    full = pl.BlockSpec((rows, kv_cols), lambda i, b: (0, 0))
    mine = pl.BlockSpec((tile, width), lambda i, b: (i, 0))
    row = pl.BlockSpec((heads, tile), lambda i, b: (0, i))
    table = pl.BlockSpec((tile, 128), lambda i, b: (i, 0))
    pair = pl.BlockSpec((peers // 2, rows, kv_cols), lambda i, b: (0, 0, 0))
    pair_shape = jax.ShapeDtypeStruct((peers // 2, rows, kv_cols), bf16)
    return pl.pallas_call(
        kernel,
        out_shape=(jax.ShapeDtypeStruct((rows, width), bf16), pair_shape, pair_shape),
        grid_spec=pltpu.PrefetchScalarGridSpec(
            num_scalar_prefetch=1,
            grid=(4,),
            in_specs=[mine, mine]
            + [full] * peers
            + [
                row,
                row,
                pl.BlockSpec((2, tile), lambda i, b: (0, i)),
                pl.BlockSpec((4, span, 1), lambda i, b: (0, 0, 0)),
                table,
                table,
            ],
            out_specs=[mine, pair, pair],
            scratch_shapes=[
                pltpu.VMEM((4, span, kv_cols), bf16),
                pltpu.VMEM((kv_heads, 4, span, HEAD_SIZE), f32),
                pltpu.VMEM((kv_heads, 4, span, HEAD_SIZE), f32),
                pltpu.VMEM((kv_heads, HEAD_SIZE, group * tile), f32),
            ],
        ),
        cost_estimate=pl.CostEstimate(
            flops=10 * rows * rows * peers * width, bytes_accessed=8 * 2**20, transcendentals=2**22
        ),
        compiler_params=pltpu.CompilerParams(vmem_limit_bytes=48 * 2**20),
        name="attend_back",
    )(bounds, query, grads, *pieces, logs, inner, query_rows, key_cols, cosine, sine)


def body(
    layer_input,
    cotangent,
    dealing,
    segments,
    lengths,
    routes,
    attention_gain,
    query_weight,
    key_projection,
    value_projection,
    output_weight,
    mixture_gain,
    router_weight,
    gate_weight,
    up_weight,
    down_weight,
):
    rows, width = layer_input.shape
    half_rows = rows // 2
    groups = lax.axis_size("fsdp")
    peers = lax.axis_size("ctx")
    here, place, side = lax.axis_index("fsdp"), lax.axis_index("ctx"), lax.axis_index("tp")
    parity = place % 2
    experts, _, hidden = gate_weight.shape
    expert_count = router_weight.shape[1]
    heads_width = query_weight.shape[1]
    kv_width = key_projection.shape[1]
    query_heads = heads_width // HEAD_SIZE
    kv_heads = kv_width // HEAD_SIZE
    scale = HEAD_SIZE ** (-0.5)

    def my_half(x):
        return lax.dynamic_slice_in_dim(x, side * half_rows, half_rows, 0)

    def other_half(x):
        return lax.dynamic_slice_in_dim(x, (1 - side) * half_rows, half_rows, 0)

    seg_row, deal_row, len_row = segments[0], dealing[0], lengths[0]
    seq_ids = jnp.arange(len_row.shape[0], dtype=jnp.int32)
    starts = jnp.sum((seg_row[:, None] < seq_ids[None, :]).astype(jnp.int32), 0)
    order = jnp.stack(
        [lax.dynamic_slice_in_dim(deal_row, (place ^ j) * rows, rows) for j in range(peers)]
    )
    rank = jnp.sum((order[:, None, :] < order[:, :, None]).astype(jnp.int32), -1)
    spots = jnp.arange(rows, dtype=jnp.int32)
    matches = rank[:, None, :] == spots[None, :, None]
    places = jnp.sum(jnp.where(matches, order[:, None, :], 0), -1)
    sorter = matches[0].astype(bf16)

    def segment_values(table, values):
        result = jnp.full(values.shape, table[0], jnp.int32)
        for s in range(1, table.shape[0]):
            result = jnp.where(values >= starts[s], table[s], result)
        return result

    begins = segment_values(starts, places)
    live = places - begins < segment_values(len_row, places)
    live_column = live[0].astype(f32)[:, None]
    live_half = my_half(live_column)
    cosine, sine = rope_tables(places[0], begins[0])
    tiles = 4
    tile = rows // tiles
    span = peers * tile
    own_info = jnp.stack([places[0], begins[0]])
    key_places = jnp.where(live, places, 2**30).reshape(peers, tiles, tile).transpose(1, 0, 2)
    block_low = jnp.min(places[:, ::tile], 0)
    block_high = jnp.max(places[:, tile - 1 :: tile], 0)
    needed = (block_low[None, :] <= places[0, tile - 1 :: tile][:, None]) & (
        block_high[None, :] >= begins[0, ::tile][:, None]
    )
    numbers = jnp.arange(tiles, dtype=jnp.int32)[None, :]
    bounds = jnp.concatenate(
        [
            jnp.min(jnp.where(needed, numbers, tiles), 1),
            jnp.max(jnp.where(needed, numbers + 1, 0), 1),
        ]
    )

    def sort_rows(x):
        return jnp.dot(sorter, x, preferred_element_type=f32).astype(bf16)

    layer_input = sort_rows(layer_input)
    cotangent = sort_rows(cotangent)

    expert_ids = jnp.arange(expert_count, dtype=jnp.int32)
    chosen = jnp.sum((routes[:, :, None] == expert_ids[None, None, :]).astype(f32), 1).astype(bf16)
    mark = (jnp.dot(sorter, chosen, preferred_element_type=f32) * (1.0 + live_column)).astype(bf16)
    small = jnp.concatenate([router_weight, attention_gain[:, None], mixture_gain[:, None]], 1)
    small = gather_small(small).reshape(groups * small.shape[0], expert_count + 2)
    router_full = small[:, :expert_count]
    first_gain = small[:, expert_count].astype(f32)[None, :]
    second_gain = small[:, expert_count + 1].astype(f32)[None, :]
    mark_mine, mark_other = my_half(mark), other_half(mark)
    marks = gather_small(jnp.concatenate([mark_mine, mark_other], 0))

    kv_full = gather_rows(jnp.concatenate([key_projection, value_projection], 1))
    query_full = lax.all_gather(query_weight, "fsdp", axis=0, tiled=True)
    output_local, kv_full = lax.optimization_barrier((output_weight, kv_full))
    output_turned = gather_small(output_local.T).reshape(width, heads_width)

    input_float = layer_input.astype(f32)
    inverse_one = lax.rsqrt(jnp.mean(input_float * input_float, -1, keepdims=True) + epsilon)
    unit_one = input_float * inverse_one
    normed_one = (unit_one * first_gain).astype(bf16)
    kv_rows = project(normed_one, kv_full, cosine, sine, kv_width, 1.0)
    kv_far = swap_far(kv_rows)
    kv_near = swap_core(kv_rows)
    pieces = [kv_rows, kv_near, kv_far, swap_core(kv_far)]
    query_rows = project(normed_one, query_full, cosine, sine, heads_width, scale)
    attended_rows, head_totals = attend(
        bounds, query_rows, pieces, own_info.T, key_places.reshape(tiles, 1, span), kv_heads
    )

    branch_part = contract_cols(other_half(attended_rows), output_turned).astype(bf16)
    branch = contract_cols(my_half(attended_rows), output_turned) + swap_tp(branch_part).astype(f32)
    middle = my_half(input_float) + branch * live_half
    inverse_two = lax.rsqrt(jnp.mean(middle * middle, -1, keepdims=True) + epsilon)
    unit_two = middle * inverse_two
    normed_two = (unit_two * second_gain).astype(bf16)

    grad_out_half = my_half(cotangent)
    all_grads = lax.all_gather(grad_out_half, ("fsdp", "tp"), axis=0, tiled=True)
    chunks = []
    if few_groups():
        for k in [0] + sorted(range(1, groups), key=lambda k: min(k, groups - k)):
            x_mine = normed_two if k == 0 else shift_fsdp(normed_two, k)
            chunks.append([k, x_mine, None, pick(marks, (here + groups - k) % groups)])
    else:
        x_mine = lax.all_gather(normed_two, "fsdp", axis=0, tiled=True)
        chunks.append([0, x_mine, None, marks.reshape(groups * rows, expert_count)])
    results = []
    g_blocks = []
    for chunk in chunks:
        k, x_mine, _, marked = chunk
        if results:
            x_mine = lax.optimization_barrier((x_mine, results[0][0]))[0]
            marked = lax.optimization_barrier((marked, results[-1][0]))[0]
        x_other = swap_tp(x_mine)
        chunk[1], chunk[2] = x_mine, x_other
        source = (here + groups - k) % groups * 2 if few_groups() else 0 * here
        g_blocks += [source + side, source + 1 - side]
        base = jnp.stack([here * experts] + g_blocks[-2:])
        results.append(
            run_experts(
                base,
                x_mine,
                x_other,
                all_grads,
                marked,
                router_full,
                gate_weight,
                up_weight,
                down_weight,
            )
        )

    hidden_acts = [r[2] for r in results]

    x_rows = [x for c in chunks for x in c[1:3]]
    g_rows = [all_grads] * (2 * len(chunks))
    gate_up_acts = [[r[3] for r in results], [r[4] for r in results]]
    chunk_rows = chunks[0][1].shape[0]

    def expert_grads(half, down_come, gate_up_come):
        x_picks = jnp.stack([half] + [0 * half] * len(x_rows))
        g_picks = jnp.stack([half] + g_blocks)
        down = weight_grads(g_picks, chunk_rows, 2, g_rows, [hidden_acts], down_come, False, hidden)
        gate_up = weight_grads(
            x_picks, chunk_rows, 1, x_rows, gate_up_acts, gate_up_come, True, hidden
        )
        return down, gate_up

    down_sent, gate_up_sent = expert_grads(1 - parity, (), ())
    down_chip, gate_up_chip = expert_grads(
        parity, [swap_core(x) for x in down_sent], [swap_core(x) for x in gate_up_sent]
    )

    own_logits = jnp.dot(normed_two, router_full, preferred_element_type=f32)
    gates = chosen_softmax(own_logits, mark_mine.astype(f32))
    if few_groups():
        came = []
        for c, res in zip(chunks, results):
            other_came = swap_tp(res[1])
            both = res[0].astype(f32) + other_came.astype(f32)
            if c[0]:
                both = shift_fsdp(both.astype(bf16), -c[0]).astype(f32)
            came.append(both)
        score = jnp.stack([res[5].T for res in results])
        score = score[:, :, :half_rows] + swap_tp(score[:, :, half_rows:])
        scores_all = jnp.zeros((groups, experts, half_rows), f32)
        for i, c in enumerate(chunks):
            k = c[0]
            back = shift_fsdp(score[i], -k) if k else score[i]
            scores_all = lax.dynamic_update_slice(scores_all, back[None], ((here + k) % groups, 0, 0))
        grad_two = sum(came[1:], came[0])
        grad_gates = scores_all.reshape(expert_count, half_rows).T
    else:
        res = results[0]
        tiled = res[5].reshape(-1, 2, ROW_TILE // 2, experts)
        score = tiled[:, 0] + swap_tp(tiled[:, 1])
        score = lax.all_to_all(
            score.reshape(groups, half_rows, experts), "fsdp", split_axis=0, concat_axis=0, tiled=True
        )
        grad_gates = score.transpose(1, 0, 2).reshape(half_rows, expert_count)
        grad_two = lax.psum_scatter(
            res[0].astype(f32) + swap_tp(res[1]).astype(f32), "fsdp", scatter_dimension=0, tiled=True
        )
    grad_gates = grad_gates * live_half
    grad_logits = (gates * (grad_gates - jnp.sum(gates * grad_gates, -1, keepdims=True))).astype(bf16)
    grad_normed_two = grad_two + contract_cols(grad_logits, router_full)
    grad_router = contract_rows(normed_two, grad_logits)
    scaled = grad_normed_two * second_gain
    grad_second_gain = jnp.sum(grad_normed_two * unit_two, 0)
    grad_middle_half = grad_out_half.astype(f32) + inverse_two * (
        scaled - unit_two * jnp.mean(scaled * unit_two, -1, keepdims=True)
    )
    grad_middle_low = grad_middle_half.astype(bf16)
    grad_middle_came = swap_tp(grad_middle_low)
    grad_middle = put_pair(side, grad_middle_low, grad_middle_came)

    down_flat = down_weight.reshape(experts * hidden, width)
    hidden_late = lax.optimization_barrier((hidden_acts, grad_middle_low))[0]
    mixture_parts = [
        jnp.dot(acts, down_flat, preferred_element_type=f32).astype(bf16) for acts in hidden_late
    ]
    grad_branch = (grad_middle * live_column.astype(bf16)).astype(bf16)

    def finish(chip, axis):
        came_far = swap_far(chip)
        total = (chip.astype(f32) + came_far.astype(f32)).astype(bf16)
        return join_halves(parity.reshape(1), total, swap_core(total), axis)

    grad_down = finish(down_chip[0], 2)
    grad_gate = finish(gate_up_chip[0], 1)

    if few_groups():
        parts, grad_middle = lax.optimization_barrier((mixture_parts, grad_middle))
        others = swap_tp(jnp.concatenate([p[half_rows:] for p in parts], 0))
    else:
        tiled = mixture_parts[0].reshape(-1, 2, ROW_TILE // 2, width)
        summed = (tiled[:, 0].astype(f32) + swap_tp(tiled[:, 1]).astype(f32)).reshape(-1, width)

    grad_attended = jnp.dot(grad_branch, output_turned, preferred_element_type=f32).astype(bf16)
    inner = jnp.sum(
        (grad_attended.astype(f32) * attended_rows.astype(f32)).reshape(rows, query_heads, HEAD_SIZE), -1
    )
    grad_query_pre, kept, sent = attend_back(
        bounds,
        query_rows,
        grad_attended,
        pieces,
        head_totals.T,
        inner.T,
        own_info,
        key_places.reshape(tiles, span, 1),
        cosine,
        sine,
        kv_heads,
        scale,
    )
    near = swap_core(sent)
    far = swap_far((kept[1].astype(f32) + near[1].astype(f32)).astype(bf16))
    grad_kv_pre = keys_back(kept, near, far, cosine, sine)
    up_chip, grad_kv_pre = lax.optimization_barrier((gate_up_chip[1], grad_kv_pre))
    grad_up = finish(up_chip, 1)
    grad_one_part = contract_cols(grad_query_pre, query_full) + contract_cols(grad_kv_pre, kv_full)
    grad_first_gain = jnp.sum(grad_one_part * unit_one, 0)
    low = lax.reduce_precision(grad_one_part, 8, 7)
    low_came = swap_tp(low.astype(bf16))
    grad_query_late, grad_kv_late, grad_branch, low = lax.optimization_barrier(
        (grad_query_pre, grad_kv_pre, grad_branch, low)
    )
    if few_groups():
        others, low_came = lax.optimization_barrier((others, low_came))
        mixture = jnp.zeros((half_rows, width), f32)
        for i, c in enumerate(chunks):
            k = c[0]
            both = parts[i][:half_rows].astype(f32) + others[i * half_rows : (i + 1) * half_rows].astype(f32)
            mixture = mixture + (shift_fsdp(both.astype(bf16), -k).astype(f32) if k else both)
    else:
        mixture = lax.psum_scatter(summed, "fsdp", scatter_dimension=0, tiled=True)
    output_half = (middle + mixture * live_half).astype(bf16)
    layer_output = contract_rows(sorter, put_pair(side, output_half, swap_tp(output_half))).astype(bf16)
    grad_normed_one = low + low_came.astype(f32)
    scaled = grad_normed_one * first_gain
    grad_input = grad_middle.astype(f32) + inverse_one * (
        scaled - unit_one * jnp.mean(scaled * unit_one, -1, keepdims=True)
    )
    coarse = lax.reduce_precision(grad_input, 8, 7)
    fine = (grad_input - coarse).astype(bf16)
    grad_input = contract_rows(sorter, coarse.astype(bf16)) + contract_rows(sorter, fine)

    shard = width // groups

    def blocks_of(whole):
        return reduce_blocks(whole.reshape(groups, shard, whole.shape[1]))

    grad_output = blocks_of(contract_rows(grad_branch, attended_rows)).T
    grad_query = blocks_of(contract_rows(normed_one, grad_query_late))
    grad_kv_w = blocks_of(contract_rows(normed_one, grad_kv_late))
    early = jnp.concatenate([grad_router.T, grad_second_gain[None, :]], 0)
    early = reduce_small(lax.optimization_barrier((early, grad_query_late))[0])
    late = reduce_small(grad_first_gain[None, :])[0]
    return (
        layer_output,
        grad_input,
        late,
        grad_query,
        grad_kv_w[:, :kv_width],
        grad_kv_w[:, kv_width:],
        grad_output,
        early[expert_count],
        early[:expert_count].T,
        grad_gate,
        grad_up,
        grad_down,
    )


def solution(mesh):
    in_specs = (
        P(("fsdp", "ctx"), None),
        P(("fsdp", "ctx"), None),
        P("fsdp", None),
        P("fsdp", None),
        P("fsdp", None),
        P(("fsdp", "ctx"), None),
        P("fsdp"),
        P("fsdp", "tp"),
        P("fsdp", "tp"),
        P("fsdp", "tp"),
        P("tp", "fsdp"),
        P("fsdp"),
        P("fsdp", None),
        P("fsdp", None, "tp"),
        P("fsdp", None, "tp"),
        P("fsdp", "tp", None),
    )
    out_specs = (
        P(("fsdp", "ctx"), None),
        P(("fsdp", "ctx"), None),
        P("fsdp"),
        P("fsdp", "tp"),
        P("fsdp", "tp"),
        P("fsdp", "tp"),
        P("tp", "fsdp"),
        P("fsdp"),
        P("fsdp", None),
        P("fsdp", None, "tp"),
        P("fsdp", None, "tp"),
        P("fsdp", "tp", None),
    )

    return jax.shard_map(body, mesh=mesh, in_specs=in_specs, out_specs=out_specs, check_vma=False)
```

profile of v0, /device:TPU:0, one launch (start us, length us, event | category | flops | bytes accessed | tf_op | source)
XLA Modules:
  0.0 755.9 jit_solution(11366535252088926879)
XLA Ops:
  10.0 4.1 collective-permute-start.1
  43.4 4.4 bitcast_select_fusion
  52.3 3.2 collective-permute-done.3
  63.9 3.4 project.3.refs_0_
  77.2 3.6 collective-permute-done.12
  81.9 14.2 %collective-permute-done.13 = bf16[256,512]{1,0:T(8,128)(2,1)S(1)} collective-permute-done((bf16[256,512]{1,0:T(8,128)(2,1)}, bf16[256,512]{1,0:T(8,128)(2,1)S(1)}, u32[]{:S(2)}, u32[]{:S(2)}) %collective-permute-start.13) | collective-permute-done | bytes 262176 | tf_op jit(solution)/shard_map/ppermute | solution.py:41
  96.2 4.0 project.2.q
  101.2 26.6 %attend.1 = (bf16[512,512]{1,0:T(8,128)(2,1)}, f32[512,8]{1,0:T(8,128)}) custom-call(s32[8]{0:T(128)} %pad_add_fusion.2.bounds_ref, bf16[512,512]{1,0:T(8,128)(2,1)} %project.2.q, bf16[512,512]{1,0:T(8,128)(2,1)} %project.3.refs_0_, bf16[512,512]{1,0:T(8,128)(2,1)} %copy-done.10, bf16[512,512]{1,0:T(8,128)(2,1)} %copy-done.8, bf16[512,512]{1,0:T(8,128)(2,1)} %copy-done.12, ...), custom_call_target="tpu_custom_call" | custom-call | flops 2147483648 | bytes 4194304 | tf_op jit(solution)/shard_map/attend/pallas_call | solution.py:528
  132.3 11.1 %collective-permute-done.15 = bf16[256,1024]{1,0:T(8,128)(2,1)S(1)} collective-permute-done((bf16[256,1024]{1,0:T(8,128)(2,1)S(1)}, bf16[256,1024]{1,0:T(8,128)(2,1)S(1)}, u32[]{:S(2)}, u32[]{:S(2)}) %collective-permute-start.15) | collective-permute-done | bytes 524320 | tf_op jit(solution)/shard_map/ppermute | solution.py:29
  144.6 3.2 collective-permute-start.18
  147.8 4.1 collective-permute-start.17
  155.8 2.8 collective-permute-start.22
  158.8 17.3 %collective-permute-start.20 = (bf16[256,1024]{1,0:T(8,128)(2,1)S(1)}, bf16[256,1024]{1,0:T(8,128)(2,1)}, u32[]{:S(2)}, u32[]{:S(2)}) collective-permute-start(bf16[256,1024]{1,0:T(8,128)(2,1)S(1)} %multiply_convert_fusion.1.x_mine.refs_1_), channel_id=1, source_target_pairs={{0,8},{8,16},{16,24},{24,0},{1,9},{9,17},{17,25},{25,1},{2,10},{10... | collective-permute-start | bytes 1572872 | tf_op jit(solution)/shard_map/ppermute | solution.py:41
  177.3 22.0 %experts.4 = (bf16[256,1024]{1,0:T(8,128)(2,1)}, bf16[256,1024]{1,0:T(8,128)(2,1)}, bf16[512,2048]{1,0:T(8,128)(2,1)}, bf16[512,2048]{1,0:T(8,128)(2,1)}, bf16[512,2048]{1,0:T(8,128)(2,1)}, /*index=5*/f32[512,8]{1,0:T(8,128)}) custom-call(s32[3]{0:T(128)} %pad_add_fusion.3.base_ref, bf16[256,1024]{1,0:T(8,128)(2,1)} %copy-done.39, ...), custom_call_target="tpu_custom_call" | custom-call | flops 10737418240 | bytes 16777216 | tf_op jit(solution)/shard_map/experts/pallas_call | solution.py:240
  200.9 3.8 fusion.96
  214.7 21.6 %experts.5 = (bf16[256,1024]{1,0:T(8,128)(2,1)}, bf16[256,1024]{1,0:T(8,128)(2,1)}, bf16[512,2048]{1,0:T(8,128)(2,1)}, bf16[512,2048]{1,0:T(8,128)(2,1)}, bf16[512,2048]{1,0:T(8,128)(2,1)}, /*index=5*/f32[512,8]{1,0:T(8,128)}) custom-call(s32[3]{0:T(128)} %pad_add_fusion.4.base_ref, bf16[256,1024]{1,0:T(8,128)(2,1)} %collective-permute-done.20.x_mine.refs_3_, ...), custom_call_target="tpu_custom_call" | custom-call | flops 10737418240 | bytes 16777216 | tf_op jit(solution)/shard_map/experts/pallas_call | solution.py:240
  239.8 21.7 %experts.6 = (bf16[256,1024]{1,0:T(8,128)(2,1)}, bf16[256,1024]{1,0:T(8,128)(2,1)}, bf16[512,2048]{1,0:T(8,128)(2,1)}, bf16[512,2048]{1,0:T(8,128)(2,1)}, bf16[512,2048]{1,0:T(8,128)(2,1)}, /*index=5*/f32[512,8]{1,0:T(8,128)}) custom-call(s32[3]{0:T(128)} %pad_add_fusion.5.base_ref, bf16[256,1024]{1,0:T(8,128)(2,1)} %collective-permute-done.22.x_mine.refs_5_, ...), custom_call_target="tpu_custom_call" | custom-call | flops 10737418240 | bytes 16777216 | tf_op jit(solution)/shard_map/experts/pallas_call | solution.py:240
  263.0 21.6 %experts.7 = (bf16[256,1024]{1,0:T(8,128)(2,1)}, bf16[256,1024]{1,0:T(8,128)(2,1)}, bf16[512,2048]{1,0:T(8,128)(2,1)}, bf16[512,2048]{1,0:T(8,128)(2,1)}, bf16[512,2048]{1,0:T(8,128)(2,1)}, /*index=5*/f32[512,8]{1,0:T(8,128)}) custom-call(s32[3]{0:T(128)} %pad_add_fusion.6.base_ref, bf16[256,1024]{1,0:T(8,128)(2,1)} %collective-permute-done.24.x_mine.refs_7_, ...), custom_call_target="tpu_custom_call" | custom-call | flops 10737418240 | bytes 16777216 | tf_op jit(solution)/shard_map/experts/pallas_call | solution.py:240
  287.8 16.6 %shard_map.247 = (bf16[8,512,256]{2,1,0:T(8,128)(2,1)}, bf16[8,512,256]{2,1,0:T(8,128)(2,1)}) custom-call(s32[9]{0:T(128)} %stack.126.refs_0_, bf16[256,1024]{1,0:T(8,128)(2,1)} %copy-done.39, bf16[256,1024]{1,0:T(8,128)(2,1)} %collective-permute-done.16.x_other.refs_2_, bf16[256,1024]{1,0:T(8,128)(2,1)} %collective-permute-done.20.x_mine.refs_3_, ...), custom_call_target="tpu_custom_call" | custom-call | flops 8589934592 | bytes 27262976 | tf_op jit(solution)/shard_map/pallas_call | solution.py:351
  304.6 11.6 %shard_map.249 = bf16[8,256,512]{2,1,0:T(8,128)(2,1)} custom-call(s32[9]{0:T(128)} %stack.128.refs_0_, bf16[2048,1024]{1,0:T(8,128)(2,1)} %all-gather.5.cloned.1.call-done.g_mine.g_other.refs_1_.refs_2_.refs_3_.refs_4_.refs_5_.refs_6_.refs_7_.refs_8_, ...), custom_call_target="tpu_custom_call" | custom-call | flops 4294967296 | bytes 14680064 | tf_op jit(solution)/shard_map/pallas_call | solution.py:351
  316.1 3.1 collective-permute-start.35
  334.2 7.9 %collective-permute-done.28 = bf16[256,1024]{1,0:T(8,128)(2,1)S(1)} collective-permute-done((bf16[256,1024]{1,0:T(8,128)(2,1)S(1)}, bf16[256,1024]{1,0:T(8,128)(2,1)S(1)}, u32[]{:S(2)}, u32[]{:S(2)}) %collective-permute-start.28) | collective-permute-done | bytes 524320 | tf_op jit(solution)/shard_map/ppermute | solution.py:41
  342.1 13.8 %collective-permute-done.30 = bf16[256,1024]{1,0:T(8,128)(2,1)S(1)} collective-permute-done((bf16[256,1024]{1,0:T(8,128)(2,1)S(1)}, bf16[256,1024]{1,0:T(8,128)(2,1)S(1)}, u32[]{:S(2)}, u32[]{:S(2)}) %collective-permute-start.30) | collective-permute-done | bytes 524320 | tf_op jit(solution)/shard_map/ppermute | solution.py:41
  355.9 20.7 %collective-permute-done.32 = bf16[256,1024]{1,0:T(8,128)(2,1)S(1)} collective-permute-done((bf16[256,1024]{1,0:T(8,128)(2,1)S(1)}, bf16[256,1024]{1,0:T(8,128)(2,1)S(1)}, u32[]{:S(2)}, u32[]{:S(2)}) %collective-permute-start.32) | collective-permute-done | bytes 524320 | tf_op jit(solution)/shard_map/ppermute | solution.py:41
  379.6 3.3 convolution_convert_fusion.5
  383.0 3.3 convolution_convert_fusion.4
  386.3 5.3 collective-permute-done.37
  394.7 2.7 copy.169
  400.8 23.5 %attend_back.1 = (bf16[512,512]{1,0:T(8,128)(2,1)S(1)}, bf16[2,512,512]{2,1,0:T(8,128)(2,1)S(1)}, bf16[2,512,512]{2,1,0:T(8,128)(2,1)}) custom-call(s32[8]{0:T(128)S(1)} %copy-done.14, bf16[512,512]{1,0:T(8,128)(2,1)S(1)} %copy-done.7, bf16[512,512]{1,0:T(8,128)(2,1)S(1)} %get-tuple-element.276.go, bf16[512,512]{1,0:T(8,128)(2,1)S(1)} %copy-done.6, ...), custom_call_target="tpu_custom_call" | custom-call | flops 5368709120 | bytes 8388608 | tf_op jit(solution)/shard_map/attend_back/pallas_call | solution.py:647
  435.3 17.2 %shard_map.248 = (bf16[8,512,256]{2,1,0:T(8,128)(2,1)}, bf16[8,512,256]{2,1,0:T(8,128)(2,1)}) custom-call(s32[9]{0:T(128)} %stack.124.refs_0_, bf16[256,1024]{1,0:T(8,128)(2,1)} %copy-done.39, bf16[256,1024]{1,0:T(8,128)(2,1)} %collective-permute-done.16.x_other.refs_2_, bf16[256,1024]{1,0:T(8,128)(2,1)} %collective-permute-done.20.x_mine.refs_3_, ...), custom_call_target="tpu_custom_call" | custom-call | flops 8589934592 | bytes 27262976 | tf_op jit(solution)/shard_map/pallas_call | solution.py:351
  452.5 12.1 %shard_map.250 = bf16[8,256,512]{2,1,0:T(8,128)(2,1)} custom-call(s32[9]{0:T(128)} %stack.127.refs_0_, bf16[2048,1024]{1,0:T(8,128)(2,1)} %all-gather.5.cloned.1.call-done.g_mine.g_other.refs_1_.refs_2_.refs_3_.refs_4_.refs_5_.refs_6_.refs_7_.refs_8_, ...), custom_call_target="tpu_custom_call" | custom-call | flops 4294967296 | bytes 14680064 | tf_op jit(solution)/shard_map/pallas_call | solution.py:351
  465.4 2.8 keys_back.1
  487.6 4.2 collective-permute-done.74
  515.2 3.3 collective-permute-done.55
  520.4 3.1 collective-permute-start.63
  523.5 7.0 collective-permute-done.56
  533.5 6.7 collective-permute-done.62
  541.3 5.4 collective-permute-done.69
  551.6 60.6 %collective-permute-done.58 = bf16[128,512]{0,1:T(8,128)(2,1)S(1)} collective-permute-done((bf16[128,512]{0,1:T(8,128)(2,1)S(1)}, bf16[128,512]{0,1:T(8,128)(2,1)S(1)}, u32[]{:S(2)}, u32[]{:S(2)}) %collective-permute-start.58) | collective-permute-done | bytes 131104 | tf_op jit(solution)/shard_map/ppermute | solution.py:37
  614.0 4.2 collective-permute-done.64
  620.0 4.5 collective-permute-done.70
  631.5 2.8 convolution_add_fusion.1
  640.6 26.7 %collective-permute-done.80 = bf16[8,512,256]{2,1,0:T(8,128)(2,1)S(1)} collective-permute-done((bf16[8,512,256]{2,1,0:T(8,128)(2,1)S(1)}, bf16[8,512,256]{2,1,0:T(8,128)(2,1)S(1)}, u32[]{:S(2)}, u32[]{:S(2)}) %collective-permute-start.80) | collective-permute-done | bytes 2097184 | tf_op jit(solution)/shard_map/ppermute | solution.py:37
  676.8 34.1 %collective-permute-done.46 = bf16[256,1024]{1,0:T(8,128)(2,1)S(1)} collective-permute-done((bf16[256,1024]{1,0:T(8,128)(2,1)S(1)}, bf16[256,1024]{1,0:T(8,128)(2,1)S(1)}, u32[]{:S(2)}, u32[]{:S(2)}) %collective-permute-start.46) | collective-permute-done | bytes 524320 | tf_op jit(solution)/shard_map/ppermute | solution.py:41
  728.4 2.7 convolution_convert_fusion
  731.1 5.9 join.3
  737.0 5.9 join.5
  742.9 6.0 join.4
  (496 shorter events, 220.5 us)
Async XLA Ops:
  7.2 89.0 %all-gather.3.cloned.1.call-start = ((), (), s32[]{:S(2)}) async-start(), calls=%async_computation | async-start | bytes 1310720 | tf_op jit(solution)/shard_map/all_gather | solution.py:776
  7.9 169.3 %all-gather.5.cloned.1.call-start = ((), (), s32[]{:S(2)}) async-start(), calls=%async_computation.1 | async-start | bytes 4718592 | tf_op jit(solution)/shard_map/all_gather | solution.py:801
  10.0 40.9 %collective-permute-start.1 = (bf16[256,34]{0,1:T(8,128)(2,1)S(1)}, bf16[256,34]{0,1:T(8,128)(2,1)}, u32[]{:S(2)}, u32[]{:S(2)}) collective-permute-start(bf16[256,34]{0,1:T(8,128)(2,1)S(1)} %get-tuple-element.247), channel_id=1, source_target_pairs={{0,16},{8,24},{16,0},{24,8},{1,17},{9,25},{17,1},{25,9},{2,18},{10... | collective-permute-start | bytes 52232 | tf_op jit(solution)/shard_map/ppermute | solution.py:41
  14.1 36.0 %collective-permute-start = (bf16[256,34]{0,1:T(8,128)(2,1)S(1)}, bf16[256,34]{0,1:T(8,128)(2,1)}, u32[]{:S(2)}, u32[]{:S(2)}) collective-permute-start(bf16[256,34]{0,1:T(8,128)(2,1)S(1)} %get-tuple-element.247), channel_id=1, source_target_pairs={{0,8},{8,16},{16,24},{24,0},{1,9},{9,17},{17,25},{25,1},{2,10},{10... | collective-permute-start | bytes 52232 | tf_op jit(solution)/shard_map/ppermute | solution.py:41
  15.7 32.8 %collective-permute-start.2 = (bf16[256,34]{0,1:T(8,128)(2,1)S(1)}, bf16[256,34]{0,1:T(8,128)(2,1)}, u32[]{:S(2)}, u32[]{:S(2)}) collective-permute-start(bf16[256,34]{0,1:T(8,128)(2,1)S(1)} %get-tuple-element.247), channel_id=1, source_target_pairs={{0,24},{8,0},{16,8},{24,16},{1,25},{9,1},{17,9},{25,17},{2,26},{10... | collective-permute-start | bytes 52232 | tf_op jit(solution)/shard_map/ppermute | solution.py:41
  20.4 36.3 %collective-permute-start.7 = (bf16[128,512]{1,0:T(8,128)(2,1)}, bf16[128,512]{1,0:T(8,128)(2,1)}, u32[]{:S(2)}, u32[]{:S(2)}) collective-permute-start(bf16[128,512]{1,0:T(8,128)(2,1)} %constant_dynamic-slice_fusion.16), channel_id=1, source_target_pairs={{0,24},{8,0},{16,8},{24,16},{1,25},{9,1},{17,9},{25,17},{2,26},{10... | collective-permute-start | bytes 393224 | tf_op jit(solution)/shard_map/ppermute | solution.py:41
  20.4 36.8 %collective-permute-start.5 = (bf16[128,512]{1,0:T(8,128)(2,1)}, bf16[128,512]{1,0:T(8,128)(2,1)}, u32[]{:S(2)}, u32[]{:S(2)}) collective-permute-start(bf16[128,512]{1,0:T(8,128)(2,1)} %constant_dynamic-slice_fusion.16), channel_id=1, source_target_pairs={{0,16},{8,24},{16,0},{24,8},{1,17},{9,25},{17,1},{25,9},{2,18},{10... | collective-permute-start | bytes 393224 | tf_op jit(solution)/shard_map/ppermute | solution.py:41
  63.9 16.9 %collective-permute-start.12 = (bf16[256,512]{1,0:T(8,128)(2,1)}, bf16[256,512]{1,0:T(8,128)(2,1)}, u32[]{:S(2)}, u32[]{:S(2)}) collective-permute-start(bf16[256,512]{1,0:T(8,128)(2,1)} %bitcast.23), channel_id=1, source_target_pairs={{0,8},{8,16},{16,24},{24,0},{1,9},{9,17},{17,25},{25,1},{2,10},{10... | collective-permute-start | bytes 786440 | tf_op jit(solution)/shard_map/ppermute | solution.py:41
  71.8 24.3 %collective-permute-start.13 = (bf16[256,512]{1,0:T(8,128)(2,1)}, bf16[256,512]{1,0:T(8,128)(2,1)S(1)}, u32[]{:S(2)}, u32[]{:S(2)}) collective-permute-start(bf16[256,512]{1,0:T(8,128)(2,1)} %bitcast.23), channel_id=1, source_target_pairs={{0,16},{8,24},{16,0},{24,8},{1,17},{9,25},{17,1},{25,9},{2,18},{10... | collective-permute-start | bytes 786440 | tf_op jit(solution)/shard_map/ppermute | solution.py:41
  73.7 22.4 %collective-permute-start.14 = (bf16[256,512]{1,0:T(8,128)(2,1)}, bf16[256,512]{1,0:T(8,128)(2,1)S(1)}, u32[]{:S(2)}, u32[]{:S(2)}) collective-permute-start(bf16[256,512]{1,0:T(8,128)(2,1)} %bitcast.23), channel_id=1, source_target_pairs={{0,24},{8,0},{16,8},{24,16},{1,25},{9,1},{17,9},{25,17},{2,26},{10... | collective-permute-start | bytes 786440 | tf_op jit(solution)/shard_map/ppermute | solution.py:41
  76.1 24.1 %collective-permute-start.9 = (bf16[512,512]{1,0:T(8,128)(2,1)S(1)}, bf16[512,512]{1,0:T(8,128)(2,1)S(1)}, u32[]{:S(2)}, u32[]{:S(2)}) collective-permute-start(bf16[512,512]{1,0:T(8,128)(2,1)S(1)} %copy-done.5), channel_id=1, source_target_pairs={{0,2},{2,0},{4,6},{6,4},{1,3},{3,1},{5,7},{7,5},{8,10},{10,8},{12,... | collective-permute-start | bytes 1572872 | tf_op jit(solution)/shard_map/ppermute | solution.py:33
  81.8 18.4 %collective-permute-start.11 = (bf16[512,512]{1,0:T(8,128)(2,1)S(1)}, bf16[512,512]{1,0:T(8,128)(2,1)S(1)}, u32[]{:S(2)}, u32[]{:S(2)}) collective-permute-start(bf16[512,512]{1,0:T(8,128)(2,1)S(1)} %collective-permute-done.10.refs_2_), channel_id=1, source_target_pairs={{0,2},{2,0},{4,6},{6,4},{1,3},{3,1},{5,7},{7,5},{8,10},{10,8},{12,... | collective-permute-start | bytes 1572872 | tf_op jit(solution)/shard_map/ppermute | solution.py:33
  144.6 31.6 %collective-permute-start.18 = (bf16[512,32]{0,1:T(8,128)(2,1)S(1)}, bf16[512,32]{0,1:T(8,128)(2,1)S(1)}, u32[]{:S(2)}, u32[]{:S(2)}) collective-permute-start(bf16[512,32]{0,1:T(8,128)(2,1)S(1)} %get-tuple-element.245), channel_id=1, source_target_pairs={{0,16},{8,24},{16,0},{24,8},{1,17},{9,25},{17,1},{25,9},{2,18},{10... | collective-permute-start | bytes 98312 | tf_op jit(solution)/shard_map/ppermute | solution.py:41
  151.9 60.2 %collective-permute-start.24 = (bf16[256,1024]{1,0:T(8,128)(2,1)S(1)}, bf16[256,1024]{1,0:T(8,128)(2,1)}, u32[]{:S(2)}, u32[]{:S(2)}) collective-permute-start(bf16[256,1024]{1,0:T(8,128)(2,1)S(1)} %multiply_convert_fusion.1.x_mine.refs_1_), channel_id=1, source_target_pairs={{0,16},{8,24},{16,0},{24,8},{1,17},{9,25},{17,1},{25,9},{2,18},{10... | collective-permute-start | bytes 1572872 | tf_op jit(solution)/shard_map/ppermute | solution.py:41
  153.4 23.9 %collective-permute-start.16 = (bf16[256,1024]{1,0:T(8,128)(2,1)S(1)}, bf16[256,1024]{1,0:T(8,128)(2,1)}, u32[]{:S(2)}, u32[]{:S(2)}) collective-permute-start(bf16[256,1024]{1,0:T(8,128)(2,1)S(1)} %multiply_convert_fusion.1.x_mine.refs_1_), channel_id=1, source_target_pairs={{0,1},{1,0},{2,3},{3,2},{4,5},{5,4},{6,7},{7,6},{8,9},{9,8},{10,11... | collective-permute-start | bytes 1572872 | tf_op jit(solution)/shard_map/ppermute | solution.py:29
  155.8 56.3 %collective-permute-start.22 = (bf16[256,1024]{1,0:T(8,128)(2,1)S(1)}, bf16[256,1024]{1,0:T(8,128)(2,1)}, u32[]{:S(2)}, u32[]{:S(2)}) collective-permute-start(bf16[256,1024]{1,0:T(8,128)(2,1)S(1)} %multiply_convert_fusion.1.x_mine.refs_1_), channel_id=1, source_target_pairs={{0,24},{8,0},{16,8},{24,16},{1,25},{9,1},{17,9},{25,17},{2,26},{10... | collective-permute-start | bytes 1572872 | tf_op jit(solution)/shard_map/ppermute | solution.py:41
  158.8 40.5 %collective-permute-start.20 = (bf16[256,1024]{1,0:T(8,128)(2,1)S(1)}, bf16[256,1024]{1,0:T(8,128)(2,1)}, u32[]{:S(2)}, u32[]{:S(2)}) collective-permute-start(bf16[256,1024]{1,0:T(8,128)(2,1)S(1)} %multiply_convert_fusion.1.x_mine.refs_1_), channel_id=1, source_target_pairs={{0,8},{8,16},{16,24},{24,0},{1,9},{9,17},{17,25},{25,1},{2,10},{10... | collective-permute-start | bytes 1572872 | tf_op jit(solution)/shard_map/ppermute | solution.py:41
  199.3 15.5 %collective-permute-start.21 = (bf16[256,1024]{1,0:T(8,128)(2,1)}, bf16[256,1024]{1,0:T(8,128)(2,1)}, u32[]{:S(2)}, u32[]{:S(2)}) collective-permute-start(bf16[256,1024]{1,0:T(8,128)(2,1)} %collective-permute-done.20.x_mine.refs_3_), channel_id=1, source_target_pairs={{0,1},{1,0},{2,3},{3,2},{4,5},{5,4},{6,7},{7,6},{8,9},{9,8},{10,11... | collective-permute-start | bytes 1572872 | tf_op jit(solution)/shard_map/ppermute | solution.py:29
  212.1 26.9 %collective-permute-start.23 = (bf16[256,1024]{1,0:T(8,128)(2,1)}, bf16[256,1024]{1,0:T(8,128)(2,1)S(1)}, u32[]{:S(2)}, u32[]{:S(2)}) collective-permute-start(bf16[256,1024]{1,0:T(8,128)(2,1)} %collective-permute-done.22.x_mine.refs_5_), channel_id=1, source_target_pairs={{0,1},{1,0},{2,3},{3,2},{4,5},{5,4},{6,7},{7,6},{8,9},{9,8},{10,11... | collective-permute-start | bytes 1572872 | tf_op jit(solution)/shard_map/ppermute | solution.py:29
  212.7 50.4 %collective-permute-start.25 = (bf16[256,1024]{1,0:T(8,128)(2,1)}, bf16[256,1024]{1,0:T(8,128)(2,1)}, u32[]{:S(2)}, u32[]{:S(2)}) collective-permute-start(bf16[256,1024]{1,0:T(8,128)(2,1)} %collective-permute-done.24.x_mine.refs_7_), channel_id=1, source_target_pairs={{0,1},{1,0},{2,3},{3,2},{4,5},{5,4},{6,7},{7,6},{8,9},{9,8},{10,11... | collective-permute-start | bytes 1572872 | tf_op jit(solution)/shard_map/ppermute | solution.py:29
  214.2 119.9 %collective-permute-start.26 = (bf16[256,1024]{1,0:T(8,128)(2,1)}, bf16[256,1024]{1,0:T(8,128)(2,1)S(1)}, u32[]{:S(2)}, u32[]{:S(2)}) collective-permute-start(bf16[256,1024]{1,0:T(8,128)(2,1)} %get-tuple-element.87), channel_id=1, source_target_pairs={{0,1},{1,0},{2,3},{3,2},{4,5},{5,4},{6,7},{7,6},{8,9},{9,8},{10,11... | collective-permute-start | bytes 1572872 | tf_op jit(solution)/shard_map/ppermute | solution.py:29
  237.4 88.9 %collective-permute-start.27 = (bf16[256,1024]{1,0:T(8,128)(2,1)}, bf16[256,1024]{1,0:T(8,128)(2,1)}, u32[]{:S(2)}, u32[]{:S(2)}) collective-permute-start(bf16[256,1024]{1,0:T(8,128)(2,1)} %get-tuple-element.88), channel_id=1, source_target_pairs={{0,1},{1,0},{2,3},{3,2},{4,5},{5,4},{6,7},{7,6},{8,9},{9,8},{10,11... | collective-permute-start | bytes 1572872 | tf_op jit(solution)/shard_map/ppermute | solution.py:29
  262.6 67.2 %collective-permute-start.29 = (bf16[256,1024]{1,0:T(8,128)(2,1)}, bf16[256,1024]{1,0:T(8,128)(2,1)}, u32[]{:S(2)}, u32[]{:S(2)}) collective-permute-start(bf16[256,1024]{1,0:T(8,128)(2,1)} %get-tuple-element.89), channel_id=1, source_target_pairs={{0,1},{1,0},{2,3},{3,2},{4,5},{5,4},{6,7},{7,6},{8,9},{9,8},{10,11... | collective-permute-start | bytes 1572872 | tf_op jit(solution)/shard_map/ppermute | solution.py:29
  285.7 18.7 %collective-permute-start.33 = (f32[4,8,256]{2,1,0:T(8,128)S(1)}, f32[4,8,256]{2,1,0:T(8,128)S(1)}, u32[]{:S(2)}, u32[]{:S(2)}) collective-permute-start(f32[4,8,256]{2,1,0:T(8,128)S(1)} %slice.184), channel_id=1, source_target_pairs={{0,1},{1,0},{2,3},{3,2},{4,5},{5,4},{6,7},{7,6},{8,9},{9,8},{10,11... | collective-permute-start | bytes 98312 | tf_op jit(solution)/shard_map/ppermute | solution.py:29
  287.4 43.6 %collective-permute-start.31 = (bf16[256,1024]{1,0:T(8,128)(2,1)}, bf16[256,1024]{1,0:T(8,128)(2,1)S(1)}, u32[]{:S(2)}, u32[]{:S(2)}) collective-permute-start(bf16[256,1024]{1,0:T(8,128)(2,1)} %get-tuple-element.91), channel_id=1, source_target_pairs={{0,1},{1,0},{2,3},{3,2},{4,5},{5,4},{6,7},{7,6},{8,9},{9,8},{10,11... | collective-permute-start | bytes 1572872 | tf_op jit(solution)/shard_map/ppermute | solution.py:29
  326.3 126.2 %collective-permute-start.82 = (bf16[8,256,512]{2,1,0:T(8,128)(2,1)}, bf16[8,256,512]{2,1,0:T(8,128)(2,1)}, u32[]{:S(2)}, u32[]{:S(2)}) collective-permute-start(bf16[8,256,512]{2,1,0:T(8,128)(2,1)} %shard_map.249), channel_id=1, source_target_pairs={{0,2},{2,0},{4,6},{6,4},{1,3},{3,1},{5,7},{7,5},{8,10},{10,8},{12,... | collective-permute-start | bytes 6291464 | tf_op jit(solution)/shard_map/ppermute | solution.py:33
  331.0 24.9 %collective-permute-start.30 = (bf16[256,1024]{1,0:T(8,128)(2,1)S(1)}, bf16[256,1024]{1,0:T(8,128)(2,1)S(1)}, u32[]{:S(2)}, u32[]{:S(2)}) collective-permute-start(bf16[256,1024]{1,0:T(8,128)(2,1)S(1)} %add_convert_fusion.10), channel_id=1, source_target_pairs={{0,8},{8,16},{16,24},{24,0},{1,9},{9,17},{17,25},{25,1},{2,10},{10... | collective-permute-start | bytes 1572872 | tf_op jit(solution)/shard_map/ppermute | solution.py:41
  331.3 45.3 %collective-permute-start.32 = (bf16[256,1024]{1,0:T(8,128)(2,1)S(1)}, bf16[256,1024]{1,0:T(8,128)(2,1)S(1)}, u32[]{:S(2)}, u32[]{:S(2)}) collective-permute-start(bf16[256,1024]{1,0:T(8,128)(2,1)S(1)} %add_convert_fusion.9), channel_id=1, source_target_pairs={{0,16},{8,24},{16,0},{24,8},{1,17},{9,25},{17,1},{25,9},{2,18},{10... | collective-permute-start | bytes 1572872 | tf_op jit(solution)/shard_map/ppermute | solution.py:41
  334.1 101.1 %collective-permute-start.39 = (bf16[8,512,256]{2,1,0:T(8,128)(2,1)}, bf16[8,512,256]{2,1,0:T(8,128)(2,1)}, u32[]{:S(2)}, u32[]{:S(2)}) collective-permute-start(bf16[8,512,256]{2,1,0:T(8,128)(2,1)} %get-tuple-element.114), channel_id=1, source_target_pairs={{0,2},{2,0},{4,6},{6,4},{1,3},{3,1},{5,7},{7,5},{8,10},{10,8},{12,... | collective-permute-start | bytes 6291464 | tf_op jit(solution)/shard_map/ppermute | solution.py:33
  342.1 93.2 %collective-permute-start.40 = (bf16[8,512,256]{2,1,0:T(8,128)(2,1)}, bf16[8,512,256]{2,1,0:T(8,128)(2,1)}, u32[]{:S(2)}, u32[]{:S(2)}) collective-permute-start(bf16[8,512,256]{2,1,0:T(8,128)(2,1)} %get-tuple-element.115), channel_id=1, source_target_pairs={{0,2},{2,0},{4,6},{6,4},{1,3},{3,1},{5,7},{7,5},{8,10},{10,8},{12,... | collective-permute-start | bytes 6291464 | tf_op jit(solution)/shard_map/ppermute | solution.py:33
  432.3 194.1 %collective-permute-start.38 = (bf16[1024,1024]{1,0:T(8,128)(2,1)}, bf16[1024,1024]{1,0:T(8,128)(2,1)}, u32[]{:S(2)}, u32[]{:S(2)}) collective-permute-start(bf16[1024,1024]{1,0:T(8,128)(2,1)} %pad_maximum_fusion), channel_id=1, source_target_pairs={{0,1},{1,0},{2,3},{3,2},{4,5},{5,4},{6,7},{7,6},{8,9},{9,8},{10,11... | collective-permute-start | bytes 6291464 | tf_op jit(solution)/shard_map/ppermute | solution.py:29
  433.9 30.7 %collective-permute-start.42 = (bf16[512,512]{1,0:T(8,128)(2,1)S(1)}, bf16[512,512]{1,0:T(8,128)(2,1)S(1)}, u32[]{:S(2)}, u32[]{:S(2)}) collective-permute-start(bf16[512,512]{1,0:T(8,128)(2,1)S(1)} %fusion.9), channel_id=1, source_target_pairs={{0,4},{2,6},{4,0},{6,2},{1,5},{3,7},{5,1},{7,3},{8,12},{10,14},{12... | collective-permute-start | bytes 1572872 | tf_op jit(solution)/shard_map/ppermute | solution.py:37
  480.1 28.7 %collective-permute-start.54 = (bf16[4,128,512]{1,2,0:T(8,128)(2,1)}, bf16[4,128,512]{1,2,0:T(8,128)(2,1)}, u32[]{:S(2)}, u32[]{:S(2)}) collective-permute-start(bf16[4,128,512]{1,2,0:T(8,128)(2,1)} %bitcast.261), channel_id=1, source_target_pairs={{0,2},{2,0},{4,6},{6,4},{1,3},{3,1},{5,7},{7,5},{8,10},{10,8},{12,... | collective-permute-start | bytes 1572872 | tf_op jit(solution)/shard_map/ppermute | solution.py:33
  514.2 16.3 %collective-permute-start.56 = (bf16[128,512]{0,1:T(8,128)(2,1)S(1)}, bf16[128,512]{0,1:T(8,128)(2,1)S(1)}, u32[]{:S(2)}, u32[]{:S(2)}) collective-permute-start(bf16[128,512]{0,1:T(8,128)(2,1)S(1)} %get-tuple-element.219), channel_id=1, source_target_pairs={{0,16},{8,24},{16,0},{24,8},{1,17},{9,25},{17,1},{25,9},{2,18},{10... | collective-permute-start | bytes 393224 | tf_op jit(solution)/shard_map/ppermute | solution.py:41
  515.0 15.5 %collective-permute-start.61 = (bf16[128,512]{0,1:T(8,128)(2,1)S(1)}, bf16[128,512]{0,1:T(8,128)(2,1)S(1)}, u32[]{:S(2)}, u32[]{:S(2)}) collective-permute-start(bf16[128,512]{0,1:T(8,128)(2,1)S(1)} %get-tuple-element.214), channel_id=1, source_target_pairs={{0,8},{8,16},{16,24},{24,0},{1,9},{9,17},{17,25},{25,1},{2,10},{10... | collective-permute-start | bytes 393224 | tf_op jit(solution)/shard_map/ppermute | solution.py:41
  518.5 109.3 %collective-permute-start.83 = (bf16[8,256,512]{2,1,0:T(8,128)(2,1)S(1)}, bf16[8,256,512]{2,1,0:T(8,128)(2,1)S(1)}, u32[]{:S(2)}, u32[]{:S(2)}) collective-permute-start(bf16[8,256,512]{2,1,0:T(8,128)(2,1)S(1)} %copy-done.25), channel_id=1, source_target_pairs={{0,4},{2,6},{4,0},{6,2},{1,5},{3,7},{5,1},{7,3},{8,12},{10,14},{12... | collective-permute-start | bytes 6291464 | tf_op jit(solution)/shard_map/ppermute | solution.py:37
  531.9 94.6 %collective-permute-start.43 = (bf16[512,1024]{1,0:T(8,128)(2,1)S(1)}, bf16[512,1024]{1,0:T(8,128)(2,1)S(1)}, u32[]{:S(2)}, u32[]{:S(2)}) collective-permute-start(bf16[512,1024]{1,0:T(8,128)(2,1)S(1)} %copy-done.54), channel_id=1, source_target_pairs={{0,1},{1,0},{2,3},{3,2},{4,5},{5,4},{6,7},{7,6},{8,9},{9,8},{10,11... | collective-permute-start | bytes 3145736 | tf_op jit(solution)/shard_map/ppermute | solution.py:29
  546.7 87.6 %collective-permute-start.78 = (bf16[8,512,256]{2,1,0:T(8,128)(2,1)S(1)}, bf16[8,512,256]{2,1,0:T(8,128)(2,1)S(1)}, u32[]{:S(2)}, u32[]{:S(2)}) collective-permute-start(bf16[8,512,256]{2,1,0:T(8,128)(2,1)S(1)} %copy-done.49), channel_id=1, source_target_pairs={{0,4},{2,6},{4,0},{6,2},{1,5},{3,7},{5,1},{7,3},{8,12},{10,14},{12... | collective-permute-start | bytes 6291464 | tf_op jit(solution)/shard_map/ppermute | solution.py:37
  549.4 62.7 %collective-permute-start.58 = (bf16[128,512]{0,1:T(8,128)(2,1)S(1)}, bf16[128,512]{0,1:T(8,128)(2,1)S(1)}, u32[]{:S(2)}, u32[]{:S(2)}) collective-permute-start(bf16[128,512]{0,1:T(8,128)(2,1)S(1)} %fusion.48), channel_id=1, source_target_pairs={{0,4},{2,6},{4,0},{6,2},{1,5},{3,7},{5,1},{7,3},{8,12},{10,14},{12... | collective-permute-start | bytes 393224 | tf_op jit(solution)/shard_map/ppermute | solution.py:37
  624.6 42.7 %collective-permute-start.80 = (bf16[8,512,256]{2,1,0:T(8,128)(2,1)S(1)}, bf16[8,512,256]{2,1,0:T(8,128)(2,1)S(1)}, u32[]{:S(2)}, u32[]{:S(2)}) collective-permute-start(bf16[8,512,256]{2,1,0:T(8,128)(2,1)S(1)} %copy-done.48), channel_id=1, source_target_pairs={{0,4},{2,6},{4,0},{6,2},{1,5},{3,7},{5,1},{7,3},{8,12},{10,14},{12... | collective-permute-start | bytes 6291464 | tf_op jit(solution)/shard_map/ppermute | solution.py:37
  626.4 43.9 %collective-permute-start.59 = (f32[128,512]{0,1:T(8,128)S(1)}, f32[128,512]{0,1:T(8,128)S(1)}, u32[]{:S(2)}, u32[]{:S(2)}) collective-permute-start(f32[128,512]{0,1:T(8,128)S(1)} %convert_add_fusion.2), channel_id=1, source_target_pairs={{0,2},{2,0},{4,6},{6,4},{1,3},{3,1},{5,7},{7,5},{8,10},{10,8},{12,... | collective-permute-start | bytes 786440 | tf_op jit(solution)/shard_map/ppermute | solution.py:33
  626.5 43.9 %collective-permute-start.65 = (f32[128,512]{0,1:T(8,128)S(1)}, f32[128,512]{0,1:T(8,128)S(1)}, u32[]{:S(2)}, u32[]{:S(2)}) collective-permute-start(f32[128,512]{0,1:T(8,128)S(1)} %convert_add_fusion.1), channel_id=1, source_target_pairs={{0,2},{2,0},{4,6},{6,4},{1,3},{3,1},{5,7},{7,5},{8,10},{10,8},{12,... | collective-permute-start | bytes 786440 | tf_op jit(solution)/shard_map/ppermute | solution.py:33
  627.9 44.3 %collective-permute-start.71 = (f32[128,512]{0,1:T(8,128)S(1)}, f32[128,512]{0,1:T(8,128)S(1)}, u32[]{:S(2)}, u32[]{:S(2)}) collective-permute-start(f32[128,512]{0,1:T(8,128)S(1)} %convert_add_fusion), channel_id=1, source_target_pairs={{0,2},{2,0},{4,6},{6,4},{1,3},{3,1},{5,7},{7,5},{8,10},{10,8},{12,... | collective-permute-start | bytes 786440 | tf_op jit(solution)/shard_map/ppermute | solution.py:33
  640.0 96.9 %collective-permute-start.84 = (bf16[8,256,512]{2,1,0:T(8,128)(2,1)}, bf16[8,256,512]{2,1,0:T(8,128)(2,1)}, u32[]{:S(2)}, u32[]{:S(2)}) collective-permute-start(bf16[8,256,512]{2,1,0:T(8,128)(2,1)} %add_convert_fusion.mine_ref), channel_id=1, source_target_pairs={{0,2},{2,0},{4,6},{6,4},{1,3},{3,1},{5,7},{7,5},{8,10},{10,8},{12,... | collective-permute-start | bytes 6291464 | tf_op jit(solution)/shard_map/ppermute | solution.py:33
  670.3 60.7 %collective-permute-start.79 = (bf16[8,512,256]{2,1,0:T(8,128)(2,1)S(1)}, bf16[8,512,256]{2,1,0:T(8,128)(2,1)}, u32[]{:S(2)}, u32[]{:S(2)}) collective-permute-start(bf16[8,512,256]{2,1,0:T(8,128)(2,1)S(1)} %add_convert_fusion.2.mine_ref), channel_id=1, source_target_pairs={{0,2},{2,0},{4,6},{6,4},{1,3},{3,1},{5,7},{7,5},{8,10},{10,8},{12,... | collective-permute-start | bytes 6291464 | tf_op jit(solution)/shard_map/ppermute | solution.py:33
  672.2 70.7 %collective-permute-start.81 = (bf16[8,512,256]{2,1,0:T(8,128)(2,1)}, bf16[8,512,256]{2,1,0:T(8,128)(2,1)}, u32[]{:S(2)}, u32[]{:S(2)}) collective-permute-start(bf16[8,512,256]{2,1,0:T(8,128)(2,1)} %add_convert_fusion.1.mine_ref), channel_id=1, source_target_pairs={{0,2},{2,0},{4,6},{6,4},{1,3},{3,1},{5,7},{7,5},{8,10},{10,8},{12,... | collective-permute-start | bytes 6291464 | tf_op jit(solution)/shard_map/ppermute | solution.py:33
  674.1 36.8 %collective-permute-start.46 = (bf16[256,1024]{1,0:T(8,128)(2,1)S(1)}, bf16[256,1024]{1,0:T(8,128)(2,1)S(1)}, u32[]{:S(2)}, u32[]{:S(2)}) collective-permute-start(bf16[256,1024]{1,0:T(8,128)(2,1)S(1)} %get-tuple-element.209), channel_id=1, source_target_pairs={{0,16},{8,24},{16,0},{24,8},{1,17},{9,25},{17,1},{25,9},{2,18},{10... | collective-permute-start | bytes 1572872 | tf_op jit(solution)/shard_map/ppermute | solution.py:41
  676.5 34.4 %collective-permute-start.45 = (bf16[256,1024]{1,0:T(8,128)(2,1)S(1)}, bf16[256,1024]{1,0:T(8,128)(2,1)S(1)}, u32[]{:S(2)}, u32[]{:S(2)}) collective-permute-start(bf16[256,1024]{1,0:T(8,128)(2,1)S(1)} %get-tuple-element.210), channel_id=1, source_target_pairs={{0,8},{8,16},{16,24},{24,0},{1,9},{9,17},{17,25},{25,1},{2,10},{10... | collective-permute-start | bytes 1572872 | tf_op jit(solution)/shard_map/ppermute | solution.py:41
  (119 other events, 1953.5 us)
Sparse Core Ops, SparseCore 0:
  9.6 37.0 all-gather.2
  49.4 91.1 all-gather.4
where the time goes:
time: 765 us; the launch traced here: 756 us
  waiting for transfers between devices  256 us (33%)
  Pallas kernels  222 us (29%)
  starting transfers between devices  112 us (15%)
  local copies, waits for them, and re-layouts  64 us (8%)
  other arithmetic  49.8 us (7%)
  matrix products  35.8 us (5%)
  between operations  15.9 us (2%)
    ppermute x39, waiting for transfers between devices, shift_fsdp(): return lax.ppermute(x, 'fsdp', shift(lax.axis_size('fsdp'), k))  131 us
    ppermute x10, waiting for transfers between devices, swap_far(): return lax.ppermute(x, 'ctx', flip(lax.axis_size('ctx'), 2))  102 us
    pallas_call x4, Pallas kernels, run_experts(): pl.pallas_call(expert_kernel, out_shape=(jax.ShapeDtypeStruct((rows, widt...  86.9 us
    ppermute x39, starting transfers between devices, shift_fsdp(): return lax.ppermute(x, 'fsdp', shift(lax.axis_size('fsdp'), k))  73.1 us
    pallas_call x4, Pallas kernels, weight_grads(): pl.pallas_call(kernel, out_shape=tuple((jax.ShapeDtypeStruct((experts,) +...  57.4 us
    pallas_call x1, Pallas kernels, attend(): pl.pallas_call(kernel, out_shape=(jax.ShapeDtypeStruct((rows, width), bf1...  26.6 us
    pallas_call x1, Pallas kernels, attend_back(): pl.pallas_call(kernel, out_shape=(jax.ShapeDtypeStruct((rows, width), bf1...  23.5 us
    ppermute x16, waiting for transfers between devices, swap_tp(): return lax.ppermute(x, 'tp', flip(lax.axis_size('tp'), 1))  21.8 us
  transfers between devices with their start and end apart: 87, of which 31 were waited for; matrix products, arithmetic and copies ran while one was open for 19% of the time, Pallas kernels for 29%

commit v1 on v0

--- a/solution.py
+++ b/solution.py
@@ -94,17 +94,26 @@
     return full
 
 
-def gather_small(x):
+def send_small(x):
+    if not few_groups():
+        return [lax.all_gather(x, "fsdp", axis=0)]
+    return [x] + [shift_fsdp(x, k) for k in range(1, lax.axis_size("fsdp"))]
+
+
+def place_small(parts):
     size = lax.axis_size("fsdp")
     if not few_groups():
-        return lax.all_gather(x, "fsdp", axis=0)
+        return parts[0]
     here = lax.axis_index("fsdp")
-    full = jnp.zeros((size,) + x.shape, x.dtype)
-    zeros = (0,) * x.ndim
+    full = jnp.zeros((size,) + parts[0].shape, parts[0].dtype)
+    zeros = (0,) * parts[0].ndim
     for k in range(size):
-        part = x if k == 0 else shift_fsdp(x, k)
-        full = lax.dynamic_update_slice(full, part[None], ((here + size - k) % size,) + zeros)
+        full = lax.dynamic_update_slice(full, parts[k][None], ((here + size - k) % size,) + zeros)
     return full
+
+
+def gather_small(x):
+    return place_small(send_small(x))
 
 
 def reduce_blocks(blocks):
@@ -775,7 +784,7 @@
     kv_full = gather_rows(jnp.concatenate([key_projection, value_projection], 1))
     query_full = lax.all_gather(query_weight, "fsdp", axis=0, tiled=True)
     output_local, kv_full = lax.optimization_barrier((output_weight, kv_full))
-    output_turned = gather_small(output_local.T).reshape(width, heads_width)
+    output_parts = send_small(output_local.T)
 
     input_float = layer_input.astype(f32)
     inverse_one = lax.rsqrt(jnp.mean(input_float * input_float, -1, keepdims=True) + epsilon)
@@ -789,6 +798,9 @@
     attended_rows, head_totals = attend(
         bounds, query_rows, pieces, own_info.T, key_places.reshape(tiles, 1, span), kv_heads
     )
+
+    output_parts, attended_rows = lax.optimization_barrier((output_parts, attended_rows))
+    output_turned = place_small(output_parts).reshape(width, heads_width)
 
     branch_part = contract_cols(other_half(attended_rows), output_turned).astype(bf16)
     branch = contract_cols(my_half(attended_rows), output_turned) + swap_tp(branch_part).astype(f32)
@@ -950,12 +962,16 @@
         (grad_query_pre, grad_kv_pre, grad_branch, low)
     )
     if few_groups():
-        others, low_came = lax.optimization_barrier((others, low_came))
-        mixture = jnp.zeros((half_rows, width), f32)
+        others = lax.optimization_barrier((others, low))[0]
+        homes = []
         for i, c in enumerate(chunks):
             k = c[0]
             both = parts[i][:half_rows].astype(f32) + others[i * half_rows : (i + 1) * half_rows].astype(f32)
-            mixture = mixture + (shift_fsdp(both.astype(bf16), -k).astype(f32) if k else both)
+            if k:
+                both = shift_fsdp(both.astype(bf16), -k).astype(f32)
+            homes.append(both)
+        homes = lax.optimization_barrier((homes, grad_down, grad_gate))[0]
+        mixture = sum(homes[1:], homes[0])
     else:
         mixture = lax.psum_scatter(summed, "fsdp", scatter_dimension=0, tiled=True)
     output_half = (middle + mixture * live_half).astype(bf16)
@@ -978,7 +994,7 @@
     grad_query = blocks_of(contract_rows(normed_one, grad_query_late))
     grad_kv_w = blocks_of(contract_rows(normed_one, grad_kv_late))
     early = jnp.concatenate([grad_router.T, grad_second_gain[None, :]], 0)
-    early = reduce_small(lax.optimization_barrier((early, grad_query_late))[0])
+    early = reduce_small(lax.optimization_barrier((early, low_came))[0])
     late = reduce_small(grad_first_gain[None, :])[0]
     return (
         layer_output,

time: 765 us -> 752 us (0.983)
  starting transfers between devices: 112 us -> 101 us
  waiting for transfers between devices: 256 us -> 246 us
  other arithmetic: 49.8 us -> 57.9 us
    ppermute x39, waiting for transfers between devices: 131 us -> 110 us  [shift_fsdp(): return lax.ppermute(x, 'fsdp', shift(lax.axis_size('fsdp'), k))]
    ppermute x16, waiting for transfers between devices: 21.8 us -> 32.4 us  [swap_tp(): return lax.ppermute(x, 'tp', flip(lax.axis_size('tp'), 1))]
    ppermute x39, starting transfers between devices: 73.1 us -> 64.4 us  [shift_fsdp(): return lax.ppermute(x, 'fsdp', shift(lax.axis_size('fsdp'), k))]
    unnamed x163 -> x187, local copies, waits for them, and re-layouts: 17.2 us -> 21.4 us
  transfers between devices with their start and end apart: 87 -> 87, of which waited for: 31 -> 26; matrix products, arithmetic and copies ran while one was open for 19% -> 19% of each run, Pallas kernels for 29% -> 29%
where the time goes in v1:
time: 752 us; the launch traced here: 743 us
  waiting for transfers between devices  246 us (33%)
  Pallas kernels  222 us (30%)
  starting transfers between devices  101 us (13%)
  local copies, waits for them, and re-layouts  62.8 us (8%)
  other arithmetic  57.9 us (8%)
  matrix products  37.5 us (5%)
  between operations  16.3 us (2%)
    ppermute x39, waiting for transfers between devices, shift_fsdp(): return lax.ppermute(x, 'fsdp', shift(lax.axis_size('fsdp'), k))  110 us
    ppermute x10, waiting for transfers between devices, swap_far(): return lax.ppermute(x, 'ctx', flip(lax.axis_size('ctx'), 2))  103 us
    pallas_call x4, Pallas kernels, run_experts(): pl.pallas_call(expert_kernel, out_shape=(jax.ShapeDtypeStruct((rows, widt...  87.2 us
    ppermute x39, starting transfers between devices, shift_fsdp(): return lax.ppermute(x, 'fsdp', shift(lax.axis_size('fsdp'), k))  64.4 us
    pallas_call x4, Pallas kernels, weight_grads(): pl.pallas_call(kernel, out_shape=tuple((jax.ShapeDtypeStruct((experts,) +...  57.4 us
    ppermute x16, waiting for transfers between devices, swap_tp(): return lax.ppermute(x, 'tp', flip(lax.axis_size('tp'), 1))  32.4 us
    pallas_call x1, Pallas kernels, attend(): pl.pallas_call(kernel, out_shape=(jax.ShapeDtypeStruct((rows, width), bf1...  26.5 us
    pallas_call x1, Pallas kernels, attend_back(): pl.pallas_call(kernel, out_shape=(jax.ShapeDtypeStruct((rows, width), bf1...  23.4 us
  transfers between devices with their start and end apart: 87, of which 26 were waited for; matrix products, arithmetic and copies ran while one was open for 19% of the time, Pallas kernels for 29%

profile of v1, /device:TPU:0, one launch (start us, length us, event | category | flops | bytes accessed | tf_op | source)
XLA Modules:
  0.0 742.9 jit_solution(7981676752231054647)
XLA Ops:
  10.5 3.1 collective-permute-start
  48.2 3.4 project.3.refs_0_
  55.4 10.5 %collective-permute-done.13.refs_2_ = bf16[512,512]{1,0:T(8,128)(2,1)S(1)} collective-permute-done((bf16[512,512]{1,0:T(8,128)(2,1)}, bf16[512,512]{1,0:T(8,128)(2,1)S(1)}, u32[]{:S(2)}, u32[]{:S(2)}) %collective-permute-start.13) | collective-permute-done | bytes 524320 | tf_op jit(solution)/shard_map/ppermute | solution.py:37
  66.6 4.4 bitcast_select_fusion
  79.5 3.6 project.2.q
  84.2 26.5 %attend.1 = (bf16[512,512]{1,0:T(8,128)(2,1)}, f32[512,8]{1,0:T(8,128)}) custom-call(s32[8]{0:T(128)} %pad_add_fusion.2.bounds_ref, bf16[512,512]{1,0:T(8,128)(2,1)} %project.2.q, bf16[512,512]{1,0:T(8,128)(2,1)} %project.3.refs_0_, bf16[512,512]{1,0:T(8,128)(2,1)} %copy-done.9, bf16[512,512]{1,0:T(8,128)(2,1)} %copy-done.7, bf16[512,512]{1,0:T(8,128)(2,1)} %copy-done.11, ...), custom_call_target="tpu_custom_call" | custom-call | flops 2147483648 | bytes 4194304 | tf_op jit(solution)/shard_map/attend/pallas_call | solution.py:537
  117.3 11.0 %collective-permute-done.15 = bf16[256,1024]{1,0:T(8,128)(2,1)S(1)} collective-permute-done((bf16[256,1024]{1,0:T(8,128)(2,1)S(1)}, bf16[256,1024]{1,0:T(8,128)(2,1)S(1)}, u32[]{:S(2)}, u32[]{:S(2)}) %collective-permute-start.15) | collective-permute-done | bytes 524320 | tf_op jit(solution)/shard_map/ppermute | solution.py:29
  129.4 12.5 %collective-permute-start.17 = (bf16[512,32]{0,1:T(8,128)(2,1)S(1)}, bf16[512,32]{0,1:T(8,128)(2,1)S(1)}, u32[]{:S(2)}, u32[]{:S(2)}) collective-permute-start(bf16[512,32]{0,1:T(8,128)(2,1)S(1)} %get-tuple-element.262), channel_id=1, source_target_pairs={{0,8},{8,16},{16,24},{24,0},{1,9},{9,17},{17,25},{25,1},{2,10},{10... | collective-permute-start | bytes 98312 | tf_op jit(solution)/shard_map/ppermute | solution.py:41
  146.8 3.8 collective-permute-start.22
  150.7 3.5 collective-permute-done.18
  158.4 22.0 %experts.4 = (bf16[256,1024]{1,0:T(8,128)(2,1)}, bf16[256,1024]{1,0:T(8,128)(2,1)}, bf16[512,2048]{1,0:T(8,128)(2,1)}, bf16[512,2048]{1,0:T(8,128)(2,1)}, bf16[512,2048]{1,0:T(8,128)(2,1)}, /*index=5*/f32[512,8]{1,0:T(8,128)}) custom-call(s32[3]{0:T(128)} %pad_add_fusion.3.base_ref, bf16[256,1024]{1,0:T(8,128)(2,1)} %copy-done.38, ...), custom_call_target="tpu_custom_call" | custom-call | flops 10737418240 | bytes 16777216 | tf_op jit(solution)/shard_map/experts/pallas_call | solution.py:249
  181.6 3.8 fusion.95
  195.8 21.7 %experts.5 = (bf16[256,1024]{1,0:T(8,128)(2,1)}, bf16[256,1024]{1,0:T(8,128)(2,1)}, bf16[512,2048]{1,0:T(8,128)(2,1)}, bf16[512,2048]{1,0:T(8,128)(2,1)}, bf16[512,2048]{1,0:T(8,128)(2,1)}, /*index=5*/f32[512,8]{1,0:T(8,128)}) custom-call(s32[3]{0:T(128)} %pad_add_fusion.4.base_ref, bf16[256,1024]{1,0:T(8,128)(2,1)} %collective-permute-done.20.x_mine.refs_3_, ...), custom_call_target="tpu_custom_call" | custom-call | flops 10737418240 | bytes 16777216 | tf_op jit(solution)/shard_map/experts/pallas_call | solution.py:249
  218.8 21.7 %experts.6 = (bf16[256,1024]{1,0:T(8,128)(2,1)}, bf16[256,1024]{1,0:T(8,128)(2,1)}, bf16[512,2048]{1,0:T(8,128)(2,1)}, bf16[512,2048]{1,0:T(8,128)(2,1)}, bf16[512,2048]{1,0:T(8,128)(2,1)}, /*index=5*/f32[512,8]{1,0:T(8,128)}) custom-call(s32[3]{0:T(128)} %pad_add_fusion.5.base_ref, bf16[256,1024]{1,0:T(8,128)(2,1)} %collective-permute-done.22.x_mine.refs_5_, ...), custom_call_target="tpu_custom_call" | custom-call | flops 10737418240 | bytes 16777216 | tf_op jit(solution)/shard_map/experts/pallas_call | solution.py:249
  241.3 21.8 %experts.7 = (bf16[256,1024]{1,0:T(8,128)(2,1)}, bf16[256,1024]{1,0:T(8,128)(2,1)}, bf16[512,2048]{1,0:T(8,128)(2,1)}, bf16[512,2048]{1,0:T(8,128)(2,1)}, bf16[512,2048]{1,0:T(8,128)(2,1)}, /*index=5*/f32[512,8]{1,0:T(8,128)}) custom-call(s32[3]{0:T(128)} %pad_add_fusion.6.base_ref, bf16[256,1024]{1,0:T(8,128)(2,1)} %collective-permute-done.24.x_mine.refs_7_, ...), custom_call_target="tpu_custom_call" | custom-call | flops 10737418240 | bytes 16777216 | tf_op jit(solution)/shard_map/experts/pallas_call | solution.py:249
  266.6 16.6 %shard_map.247 = (bf16[8,512,256]{2,1,0:T(8,128)(2,1)}, bf16[8,512,256]{2,1,0:T(8,128)(2,1)}) custom-call(s32[9]{0:T(128)} %stack.126.refs_0_, bf16[256,1024]{1,0:T(8,128)(2,1)} %copy-done.38, bf16[256,1024]{1,0:T(8,128)(2,1)} %collective-permute-done.16.x_other.refs_2_, bf16[256,1024]{1,0:T(8,128)(2,1)} %collective-permute-done.20.x_mine.refs_3_, ...), custom_call_target="tpu_custom_call" | custom-call | flops 8589934592 | bytes 27262976 | tf_op jit(solution)/shard_map/pallas_call | solution.py:360
  283.3 11.6 %shard_map.249 = bf16[8,256,512]{2,1,0:T(8,128)(2,1)} custom-call(s32[9]{0:T(128)} %stack.128.refs_0_, bf16[2048,1024]{1,0:T(8,128)(2,1)} %all-gather.5.cloned.1.call-done.g_mine.g_other.refs_1_.refs_2_.refs_3_.refs_4_.refs_5_.refs_6_.refs_7_.refs_8_, ...), custom_call_target="tpu_custom_call" | custom-call | flops 4294967296 | bytes 14680064 | tf_op jit(solution)/shard_map/pallas_call | solution.py:360
  296.9 4.2 collective-permute-done.35
  301.8 3.8 collective-permute-done.36
  312.8 21.1 %collective-permute-done.28 = bf16[256,1024]{1,0:T(8,128)(2,1)S(1)} collective-permute-done((bf16[256,1024]{1,0:T(8,128)(2,1)S(1)}, bf16[256,1024]{1,0:T(8,128)(2,1)S(1)}, u32[]{:S(2)}, u32[]{:S(2)}) %collective-permute-start.28) | collective-permute-done | bytes 524320 | tf_op jit(solution)/shard_map/ppermute | solution.py:41
  333.9 20.4 %collective-permute-done.32 = bf16[256,1024]{1,0:T(8,128)(2,1)S(1)} collective-permute-done((bf16[256,1024]{1,0:T(8,128)(2,1)S(1)}, bf16[256,1024]{1,0:T(8,128)(2,1)S(1)}, u32[]{:S(2)}, u32[]{:S(2)}) %collective-permute-start.32) | collective-permute-done | bytes 524320 | tf_op jit(solution)/shard_map/ppermute | solution.py:41
  357.9 3.4 convolution_convert_fusion.2
  361.3 3.3 convolution_convert_fusion.3
  364.6 5.5 collective-permute-done.37
  380.4 23.4 %attend_back.1 = (bf16[512,512]{1,0:T(8,128)(2,1)S(1)}, bf16[2,512,512]{2,1,0:T(8,128)(2,1)S(1)}, bf16[2,512,512]{2,1,0:T(8,128)(2,1)}) custom-call(s32[8]{0:T(128)S(1)} %copy-done.13, bf16[512,512]{1,0:T(8,128)(2,1)S(1)} %copy-done.6, bf16[512,512]{1,0:T(8,128)(2,1)S(1)} %get-tuple-element.293.go, bf16[512,512]{1,0:T(8,128)(2,1)S(1)} %copy-done.5, ...), custom_call_target="tpu_custom_call" | custom-call | flops 5368709120 | bytes 8388608 | tf_op jit(solution)/shard_map/attend_back/pallas_call | solution.py:656
  415.0 17.2 %shard_map.248 = (bf16[8,512,256]{2,1,0:T(8,128)(2,1)}, bf16[8,512,256]{2,1,0:T(8,128)(2,1)}) custom-call(s32[9]{0:T(128)} %stack.124.refs_0_, bf16[256,1024]{1,0:T(8,128)(2,1)} %copy-done.38, bf16[256,1024]{1,0:T(8,128)(2,1)} %collective-permute-done.16.x_other.refs_2_, bf16[256,1024]{1,0:T(8,128)(2,1)} %collective-permute-done.20.x_mine.refs_3_, ...), custom_call_target="tpu_custom_call" | custom-call | flops 8589934592 | bytes 27262976 | tf_op jit(solution)/shard_map/pallas_call | solution.py:360
  432.4 12.0 %shard_map.250 = bf16[8,256,512]{2,1,0:T(8,128)(2,1)} custom-call(s32[9]{0:T(128)} %stack.127.refs_0_, bf16[2048,1024]{1,0:T(8,128)(2,1)} %all-gather.5.cloned.1.call-done.g_mine.g_other.refs_1_.refs_2_.refs_3_.refs_4_.refs_5_.refs_6_.refs_7_.refs_8_, ...), custom_call_target="tpu_custom_call" | custom-call | flops 4294967296 | bytes 14680064 | tf_op jit(solution)/shard_map/pallas_call | solution.py:360
  444.5 2.9 keys_back.1
  449.3 3.2 reduce-precision_convert_fusion.2
  475.8 3.5 collective-permute-start.72
  482.4 3.6 add_convert_fusion.4
  490.5 5.5 collective-permute-done.74
  496.1 3.5 collective-permute-start.60
  501.8 5.5 collective-permute-done.68
  509.4 4.3 collective-permute-done.61
  517.4 85.6 %collective-permute-done.75 = bf16[128,512]{0,1:T(8,128)(2,1)S(1)} collective-permute-done((bf16[128,512]{0,1:T(8,128)(2,1)S(1)}, bf16[128,512]{0,1:T(8,128)(2,1)S(1)}, u32[]{:S(2)}, u32[]{:S(2)}) %collective-permute-start.75) | collective-permute-done | bytes 131104 | tf_op jit(solution)/shard_map/ppermute | solution.py:37
  604.8 3.2 collective-permute-done.69
  609.7 3.2 collective-permute-done.63
  618.2 3.4 fusion.4
  624.2 3.9 convolution_add_fusion.1
  634.8 4.3 collective-permute-done.77
  639.2 4.8 collective-permute-done.43
  650.6 10.1 %collective-permute-done.44 = bf16[256,1024]{1,0:T(8,128)(2,1)S(1)} collective-permute-done((bf16[256,1024]{1,0:T(8,128)(2,1)S(1)}, bf16[256,1024]{1,0:T(8,128)(2,1)S(1)}, u32[]{:S(2)}, u32[]{:S(2)}) %collective-permute-start.44) | collective-permute-done | bytes 524320 | tf_op jit(solution)/shard_map/ppermute | solution.py:41
  662.4 19.5 %collective-permute-done.45 = bf16[256,1024]{1,0:T(8,128)(2,1)S(1)} collective-permute-done((bf16[256,1024]{1,0:T(8,128)(2,1)S(1)}, bf16[256,1024]{1,0:T(8,128)(2,1)S(1)}, u32[]{:S(2)}, u32[]{:S(2)}) %collective-permute-start.45) | collective-permute-done | bytes 524320 | tf_op jit(solution)/shard_map/ppermute | solution.py:41
  696.5 5.9 join.4
  703.3 5.9 join.3
  718.1 9.0 %collective-permute-done.51 = bf16[256,1024]{1,0:T(8,128)(2,1)S(1)} collective-permute-done((bf16[256,1024]{1,0:T(8,128)(2,1)S(1)}, bf16[256,1024]{1,0:T(8,128)(2,1)S(1)}, u32[]{:S(2)}, u32[]{:S(2)}) %collective-permute-start.51) | collective-permute-done | bytes 524320 | tf_op jit(solution)/shard_map/ppermute | solution.py:29
  729.8 6.0 join.5
  (524 shorter events, 214.0 us)
Async XLA Ops:
  7.2 72.3 %all-gather.3.cloned.1.call-start = ((), (), s32[]{:S(2)}) async-start(), calls=%async_computation | async-start | bytes 1310720 | tf_op jit(solution)/shard_map/all_gather | solution.py:785
  7.9 150.4 %all-gather.5.cloned.1.call-start = ((), (), s32[]{:S(2)}) async-start(), calls=%async_computation.1 | async-start | bytes 4718592 | tf_op jit(solution)/shard_map/all_gather | solution.py:813
  10.5 31.4 %collective-permute-start = (bf16[128,512]{1,0:T(8,128)(2,1)}, bf16[128,512]{1,0:T(8,128)(2,1)}, u32[]{:S(2)}, u32[]{:S(2)}) collective-permute-start(bf16[128,512]{1,0:T(8,128)(2,1)} %constant_dynamic-slice_fusion.16), channel_id=1, source_target_pairs={{0,8},{8,16},{16,24},{24,0},{1,9},{9,17},{17,25},{25,1},{2,10},{10... | collective-permute-start | bytes 393224 | tf_op jit(solution)/shard_map/ppermute | solution.py:41
  13.6 29.7 %collective-permute-start.2 = (bf16[128,512]{1,0:T(8,128)(2,1)}, bf16[128,512]{1,0:T(8,128)(2,1)S(1)}, u32[]{:S(2)}, u32[]{:S(2)}) collective-permute-start(bf16[128,512]{1,0:T(8,128)(2,1)} %constant_dynamic-slice_fusion.16), channel_id=1, source_target_pairs={{0,16},{8,24},{16,0},{24,8},{1,17},{9,25},{17,1},{25,9},{2,18},{10... | collective-permute-start | bytes 393224 | tf_op jit(solution)/shard_map/ppermute | solution.py:41
  18.8 19.5 %collective-permute-start.9 = (bf16[256,34]{0,1:T(8,128)(2,1)}, bf16[256,34]{0,1:T(8,128)(2,1)}, u32[]{:S(2)}, u32[]{:S(2)}) collective-permute-start(bf16[256,34]{0,1:T(8,128)(2,1)} %get-tuple-element.264), channel_id=1, source_target_pairs={{0,8},{8,16},{16,24},{24,0},{1,9},{9,17},{17,25},{25,1},{2,10},{10... | collective-permute-start | bytes 52232 | tf_op jit(solution)/shard_map/ppermute | solution.py:41
  18.8 20.9 %collective-permute-start.10 = (bf16[256,34]{0,1:T(8,128)(2,1)}, bf16[256,34]{0,1:T(8,128)(2,1)}, u32[]{:S(2)}, u32[]{:S(2)}) collective-permute-start(bf16[256,34]{0,1:T(8,128)(2,1)} %get-tuple-element.264), channel_id=1, source_target_pairs={{0,16},{8,24},{16,0},{24,8},{1,17},{9,25},{17,1},{25,9},{2,18},{10... | collective-permute-start | bytes 52232 | tf_op jit(solution)/shard_map/ppermute | solution.py:41
  20.7 19.9 %collective-permute-start.11 = (bf16[256,34]{0,1:T(8,128)(2,1)}, bf16[256,34]{0,1:T(8,128)(2,1)}, u32[]{:S(2)}, u32[]{:S(2)}) collective-permute-start(bf16[256,34]{0,1:T(8,128)(2,1)} %get-tuple-element.264), channel_id=1, source_target_pairs={{0,24},{8,0},{16,8},{24,16},{1,25},{9,1},{17,9},{25,17},{2,26},{10... | collective-permute-start | bytes 52232 | tf_op jit(solution)/shard_map/ppermute | solution.py:41
  55.3 27.9 %collective-permute-start.12 = (bf16[512,512]{1,0:T(8,128)(2,1)}, bf16[512,512]{1,0:T(8,128)(2,1)S(1)}, u32[]{:S(2)}, u32[]{:S(2)}) collective-permute-start(bf16[512,512]{1,0:T(8,128)(2,1)} %project.3.refs_0_), channel_id=1, source_target_pairs={{0,2},{2,0},{4,6},{6,4},{1,3},{3,1},{5,7},{7,5},{8,10},{10,8},{12,... | collective-permute-start | bytes 1572872 | tf_op jit(solution)/shard_map/ppermute | solution.py:33
  65.9 17.3 %collective-permute-start.14 = (bf16[512,512]{1,0:T(8,128)(2,1)S(1)}, bf16[512,512]{1,0:T(8,128)(2,1)S(1)}, u32[]{:S(2)}, u32[]{:S(2)}) collective-permute-start(bf16[512,512]{1,0:T(8,128)(2,1)S(1)} %collective-permute-done.13.refs_2_), channel_id=1, source_target_pairs={{0,2},{2,0},{4,6},{6,4},{1,3},{3,1},{5,7},{7,5},{8,10},{10,8},{12,... | collective-permute-start | bytes 1572872 | tf_op jit(solution)/shard_map/ppermute | solution.py:33
  72.1 38.6 %collective-permute-start.6 = (bf16[256,512]{1,0:T(8,128)(2,1)S(1)}, bf16[256,512]{1,0:T(8,128)(2,1)}, u32[]{:S(2)}, u32[]{:S(2)}) collective-permute-start(bf16[256,512]{1,0:T(8,128)(2,1)S(1)} %bitcast.260), channel_id=1, source_target_pairs={{0,8},{8,16},{16,24},{24,0},{1,9},{9,17},{17,25},{25,1},{2,10},{10... | collective-permute-start | bytes 786440 | tf_op jit(solution)/shard_map/ppermute | solution.py:41
  73.2 37.5 %collective-permute-start.7 = (bf16[256,512]{1,0:T(8,128)(2,1)S(1)}, bf16[256,512]{1,0:T(8,128)(2,1)}, u32[]{:S(2)}, u32[]{:S(2)}) collective-permute-start(bf16[256,512]{1,0:T(8,128)(2,1)S(1)} %bitcast.261), channel_id=1, source_target_pairs={{0,16},{8,24},{16,0},{24,8},{1,17},{9,25},{17,1},{25,9},{2,18},{10... | collective-permute-start | bytes 786440 | tf_op jit(solution)/shard_map/ppermute | solution.py:41
  75.4 35.3 %collective-permute-start.8 = (bf16[256,512]{1,0:T(8,128)(2,1)S(1)}, bf16[256,512]{1,0:T(8,128)(2,1)}, u32[]{:S(2)}, u32[]{:S(2)}) collective-permute-start(bf16[256,512]{1,0:T(8,128)(2,1)S(1)} %bitcast.262), channel_id=1, source_target_pairs={{0,24},{8,0},{16,8},{24,16},{1,25},{9,1},{17,9},{25,17},{2,26},{10... | collective-permute-start | bytes 786440 | tf_op jit(solution)/shard_map/ppermute | solution.py:41
  129.4 17.4 %collective-permute-start.17 = (bf16[512,32]{0,1:T(8,128)(2,1)S(1)}, bf16[512,32]{0,1:T(8,128)(2,1)S(1)}, u32[]{:S(2)}, u32[]{:S(2)}) collective-permute-start(bf16[512,32]{0,1:T(8,128)(2,1)S(1)} %get-tuple-element.262), channel_id=1, source_target_pairs={{0,8},{8,16},{16,24},{24,0},{1,9},{9,17},{17,25},{25,1},{2,10},{10... | collective-permute-start | bytes 98312 | tf_op jit(solution)/shard_map/ppermute | solution.py:41
  145.7 34.6 %collective-permute-start.20 = (bf16[256,1024]{1,0:T(8,128)(2,1)S(1)}, bf16[256,1024]{1,0:T(8,128)(2,1)}, u32[]{:S(2)}, u32[]{:S(2)}) collective-permute-start(bf16[256,1024]{1,0:T(8,128)(2,1)S(1)} %multiply_convert_fusion.1.x_mine.refs_1_), channel_id=1, source_target_pairs={{0,8},{8,16},{16,24},{24,0},{1,9},{9,17},{17,25},{25,1},{2,10},{10... | collective-permute-start | bytes 1572872 | tf_op jit(solution)/shard_map/ppermute | solution.py:41
  146.8 45.0 %collective-permute-start.22 = (bf16[256,1024]{1,0:T(8,128)(2,1)S(1)}, bf16[256,1024]{1,0:T(8,128)(2,1)}, u32[]{:S(2)}, u32[]{:S(2)}) collective-permute-start(bf16[256,1024]{1,0:T(8,128)(2,1)S(1)} %multiply_convert_fusion.1.x_mine.refs_1_), channel_id=1, source_target_pairs={{0,24},{8,0},{16,8},{24,16},{1,25},{9,1},{17,9},{25,17},{2,26},{10... | collective-permute-start | bytes 1572872 | tf_op jit(solution)/shard_map/ppermute | solution.py:41
  154.2 38.5 %collective-permute-start.24 = (bf16[256,1024]{1,0:T(8,128)(2,1)S(1)}, bf16[256,1024]{1,0:T(8,128)(2,1)}, u32[]{:S(2)}, u32[]{:S(2)}) collective-permute-start(bf16[256,1024]{1,0:T(8,128)(2,1)S(1)} %multiply_convert_fusion.1.x_mine.refs_1_), channel_id=1, source_target_pairs={{0,16},{8,24},{16,0},{24,8},{1,17},{9,25},{17,1},{25,9},{2,18},{10... | collective-permute-start | bytes 1572872 | tf_op jit(solution)/shard_map/ppermute | solution.py:41
  180.3 15.4 %collective-permute-start.21 = (bf16[256,1024]{1,0:T(8,128)(2,1)}, bf16[256,1024]{1,0:T(8,128)(2,1)}, u32[]{:S(2)}, u32[]{:S(2)}) collective-permute-start(bf16[256,1024]{1,0:T(8,128)(2,1)} %collective-permute-done.20.x_mine.refs_3_), channel_id=1, source_target_pairs={{0,1},{1,0},{2,3},{3,2},{4,5},{5,4},{6,7},{7,6},{8,9},{9,8},{10,11... | collective-permute-start | bytes 1572872 | tf_op jit(solution)/shard_map/ppermute | solution.py:29
  191.8 27.0 %collective-permute-start.23 = (bf16[256,1024]{1,0:T(8,128)(2,1)}, bf16[256,1024]{1,0:T(8,128)(2,1)}, u32[]{:S(2)}, u32[]{:S(2)}) collective-permute-start(bf16[256,1024]{1,0:T(8,128)(2,1)} %collective-permute-done.22.x_mine.refs_5_), channel_id=1, source_target_pairs={{0,1},{1,0},{2,3},{3,2},{4,5},{5,4},{6,7},{7,6},{8,9},{9,8},{10,11... | collective-permute-start | bytes 1572872 | tf_op jit(solution)/shard_map/ppermute | solution.py:29
  192.7 48.7 %collective-permute-start.25 = (bf16[256,1024]{1,0:T(8,128)(2,1)}, bf16[256,1024]{1,0:T(8,128)(2,1)}, u32[]{:S(2)}, u32[]{:S(2)}) collective-permute-start(bf16[256,1024]{1,0:T(8,128)(2,1)} %collective-permute-done.24.x_mine.refs_7_), channel_id=1, source_target_pairs={{0,1},{1,0},{2,3},{3,2},{4,5},{5,4},{6,7},{7,6},{8,9},{9,8},{10,11... | collective-permute-start | bytes 1572872 | tf_op jit(solution)/shard_map/ppermute | solution.py:29
  194.9 117.8 %collective-permute-start.26 = (bf16[256,1024]{1,0:T(8,128)(2,1)}, bf16[256,1024]{1,0:T(8,128)(2,1)}, u32[]{:S(2)}, u32[]{:S(2)}) collective-permute-start(bf16[256,1024]{1,0:T(8,128)(2,1)} %get-tuple-element.100), channel_id=1, source_target_pairs={{0,1},{1,0},{2,3},{3,2},{4,5},{5,4},{6,7},{7,6},{8,9},{9,8},{10,11... | collective-permute-start | bytes 1572872 | tf_op jit(solution)/shard_map/ppermute | solution.py:29
  217.5 88.2 %collective-permute-start.27 = (bf16[256,1024]{1,0:T(8,128)(2,1)}, bf16[256,1024]{1,0:T(8,128)(2,1)}, u32[]{:S(2)}, u32[]{:S(2)}) collective-permute-start(bf16[256,1024]{1,0:T(8,128)(2,1)} %get-tuple-element.101), channel_id=1, source_target_pairs={{0,1},{1,0},{2,3},{3,2},{4,5},{5,4},{6,7},{7,6},{8,9},{9,8},{10,11... | collective-permute-start | bytes 1572872 | tf_op jit(solution)/shard_map/ppermute | solution.py:29
  240.5 68.6 %collective-permute-start.29 = (bf16[256,1024]{1,0:T(8,128)(2,1)}, bf16[256,1024]{1,0:T(8,128)(2,1)}, u32[]{:S(2)}, u32[]{:S(2)}) collective-permute-start(bf16[256,1024]{1,0:T(8,128)(2,1)} %get-tuple-element.102), channel_id=1, source_target_pairs={{0,1},{1,0},{2,3},{3,2},{4,5},{5,4},{6,7},{7,6},{8,9},{9,8},{10,11... | collective-permute-start | bytes 1572872 | tf_op jit(solution)/shard_map/ppermute | solution.py:29
  263.1 47.3 %collective-permute-start.31 = (bf16[256,1024]{1,0:T(8,128)(2,1)}, bf16[256,1024]{1,0:T(8,128)(2,1)}, u32[]{:S(2)}, u32[]{:S(2)}) collective-permute-start(bf16[256,1024]{1,0:T(8,128)(2,1)} %get-tuple-element.104), channel_id=1, source_target_pairs={{0,1},{1,0},{2,3},{3,2},{4,5},{5,4},{6,7},{7,6},{8,9},{9,8},{10,11... | collective-permute-start | bytes 1572872 | tf_op jit(solution)/shard_map/ppermute | solution.py:29
  265.7 17.4 %collective-permute-start.33 = (f32[4,8,256]{2,1,0:T(8,128)S(1)}, f32[4,8,256]{2,1,0:T(8,128)S(1)}, u32[]{:S(2)}, u32[]{:S(2)}) collective-permute-start(f32[4,8,256]{2,1,0:T(8,128)S(1)} %slice.184), channel_id=1, source_target_pairs={{0,1},{1,0},{2,3},{3,2},{4,5},{5,4},{6,7},{7,6},{8,9},{9,8},{10,11... | collective-permute-start | bytes 98312 | tf_op jit(solution)/shard_map/ppermute | solution.py:29
  305.7 109.3 %collective-permute-start.39 = (bf16[8,512,256]{2,1,0:T(8,128)(2,1)}, bf16[8,512,256]{2,1,0:T(8,128)(2,1)}, u32[]{:S(2)}, u32[]{:S(2)}) collective-permute-start(bf16[8,512,256]{2,1,0:T(8,128)(2,1)} %get-tuple-element.127), channel_id=1, source_target_pairs={{0,2},{2,0},{4,6},{6,4},{1,3},{3,1},{5,7},{7,5},{8,10},{10,8},{12,... | collective-permute-start | bytes 6291464 | tf_op jit(solution)/shard_map/ppermute | solution.py:33
  307.0 26.9 %collective-permute-start.28 = (bf16[256,1024]{1,0:T(8,128)(2,1)S(1)}, bf16[256,1024]{1,0:T(8,128)(2,1)S(1)}, u32[]{:S(2)}, u32[]{:S(2)}) collective-permute-start(bf16[256,1024]{1,0:T(8,128)(2,1)S(1)} %add_convert_fusion.11), channel_id=1, source_target_pairs={{0,24},{8,0},{16,8},{24,16},{1,25},{9,1},{17,9},{25,17},{2,26},{10... | collective-permute-start | bytes 1572872 | tf_op jit(solution)/shard_map/ppermute | solution.py:41
  310.3 23.5 %collective-permute-start.30 = (bf16[256,1024]{1,0:T(8,128)(2,1)S(1)}, bf16[256,1024]{1,0:T(8,128)(2,1)S(1)}, u32[]{:S(2)}, u32[]{:S(2)}) collective-permute-start(bf16[256,1024]{1,0:T(8,128)(2,1)S(1)} %add_convert_fusion.10), channel_id=1, source_target_pairs={{0,8},{8,16},{16,24},{24,0},{1,9},{9,17},{17,25},{25,1},{2,10},{10... | collective-permute-start | bytes 1572872 | tf_op jit(solution)/shard_map/ppermute | solution.py:41
  311.7 42.6 %collective-permute-start.32 = (bf16[256,1024]{1,0:T(8,128)(2,1)S(1)}, bf16[256,1024]{1,0:T(8,128)(2,1)S(1)}, u32[]{:S(2)}, u32[]{:S(2)}) collective-permute-start(bf16[256,1024]{1,0:T(8,128)(2,1)S(1)} %add_convert_fusion.9), channel_id=1, source_target_pairs={{0,16},{8,24},{16,0},{24,8},{1,17},{9,25},{17,1},{25,9},{2,18},{10... | collective-permute-start | bytes 1572872 | tf_op jit(solution)/shard_map/ppermute | solution.py:41
  312.7 102.3 %collective-permute-start.40 = (bf16[8,512,256]{2,1,0:T(8,128)(2,1)}, bf16[8,512,256]{2,1,0:T(8,128)(2,1)}, u32[]{:S(2)}, u32[]{:S(2)}) collective-permute-start(bf16[8,512,256]{2,1,0:T(8,128)(2,1)} %get-tuple-element.128), channel_id=1, source_target_pairs={{0,2},{2,0},{4,6},{6,4},{1,3},{3,1},{5,7},{7,5},{8,10},{10,8},{12,... | collective-permute-start | bytes 6291464 | tf_op jit(solution)/shard_map/ppermute | solution.py:33
  333.9 98.6 %collective-permute-start.46 = (bf16[8,256,512]{2,1,0:T(8,128)(2,1)}, bf16[8,256,512]{2,1,0:T(8,128)(2,1)}, u32[]{:S(2)}, u32[]{:S(2)}) collective-permute-start(bf16[8,256,512]{2,1,0:T(8,128)(2,1)} %shard_map.249), channel_id=1, source_target_pairs={{0,2},{2,0},{4,6},{6,4},{1,3},{3,1},{5,7},{7,5},{8,10},{10,8},{12,... | collective-permute-start | bytes 6291464 | tf_op jit(solution)/shard_map/ppermute | solution.py:33
  411.7 64.1 %collective-permute-start.38 = (bf16[1024,1024]{1,0:T(8,128)(2,1)}, bf16[1024,1024]{1,0:T(8,128)(2,1)}, u32[]{:S(2)}, u32[]{:S(2)}) collective-permute-start(bf16[1024,1024]{1,0:T(8,128)(2,1)} %pad_maximum_fusion), channel_id=1, source_target_pairs={{0,1},{1,0},{2,3},{3,2},{4,5},{5,4},{6,7},{7,6},{8,9},{9,8},{10,11... | collective-permute-start | bytes 6291464 | tf_op jit(solution)/shard_map/ppermute | solution.py:29
  413.1 31.4 %collective-permute-start.42 = (bf16[512,512]{1,0:T(8,128)(2,1)S(1)}, bf16[512,512]{1,0:T(8,128)(2,1)}, u32[]{:S(2)}, u32[]{:S(2)}) collective-permute-start(bf16[512,512]{1,0:T(8,128)(2,1)S(1)} %fusion.9), channel_id=1, source_target_pairs={{0,4},{2,6},{4,0},{6,2},{1,5},{3,7},{5,1},{7,3},{8,12},{10,14},{12... | collective-permute-start | bytes 1572872 | tf_op jit(solution)/shard_map/ppermute | solution.py:37
  432.2 183.7 %collective-permute-start.49 = (bf16[8,512,256]{2,1,0:T(8,128)(2,1)}, bf16[8,512,256]{2,1,0:T(8,128)(2,1)}, u32[]{:S(2)}, u32[]{:S(2)}) collective-permute-start(bf16[8,512,256]{2,1,0:T(8,128)(2,1)} %get-tuple-element.135), channel_id=1, source_target_pairs={{0,4},{2,6},{4,0},{6,2},{1,5},{3,7},{5,1},{7,3},{8,12},{10,14},{12... | collective-permute-start | bytes 6291464 | tf_op jit(solution)/shard_map/ppermute | solution.py:37
  452.5 160.6 %collective-permute-start.52 = (bf16[512,1024]{1,0:T(8,128)(2,1)}, bf16[512,1024]{1,0:T(8,128)(2,1)}, u32[]{:S(2)}, u32[]{:S(2)}) collective-permute-start(bf16[512,1024]{1,0:T(8,128)(2,1)} %get-tuple-element.222), channel_id=1, source_target_pairs={{0,1},{1,0},{2,3},{3,2},{4,5},{5,4},{6,7},{7,6},{8,9},{9,8},{10,11... | collective-permute-start | bytes 3145736 | tf_op jit(solution)/shard_map/ppermute | solution.py:29
  507.6 114.0 %collective-permute-start.47 = (bf16[8,256,512]{2,1,0:T(8,128)(2,1)S(1)}, bf16[8,256,512]{2,1,0:T(8,128)(2,1)S(1)}, u32[]{:S(2)}, u32[]{:S(2)}) collective-permute-start(bf16[8,256,512]{2,1,0:T(8,128)(2,1)S(1)} %copy-done.28), channel_id=1, source_target_pairs={{0,4},{2,6},{4,0},{6,2},{1,5},{3,7},{5,1},{7,3},{8,12},{10,14},{12... | collective-permute-start | bytes 6291464 | tf_op jit(solution)/shard_map/ppermute | solution.py:37
  513.7 133.7 %collective-permute-start.83 = (bf16[8,512,256]{2,1,0:T(8,128)(2,1)S(1)}, bf16[8,512,256]{2,1,0:T(8,128)(2,1)S(1)}, u32[]{:S(2)}, u32[]{:S(2)}) collective-permute-start(bf16[8,512,256]{2,1,0:T(8,128)(2,1)S(1)} %copy-done.50), channel_id=1, source_target_pairs={{0,4},{2,6},{4,0},{6,2},{1,5},{3,7},{5,1},{7,3},{8,12},{10,14},{12... | collective-permute-start | bytes 6291464 | tf_op jit(solution)/shard_map/ppermute | solution.py:37
  515.5 87.5 %collective-permute-start.75 = (bf16[128,512]{0,1:T(8,128)(2,1)S(1)}, bf16[128,512]{0,1:T(8,128)(2,1)S(1)}, u32[]{:S(2)}, u32[]{:S(2)}) collective-permute-start(bf16[128,512]{0,1:T(8,128)(2,1)S(1)} %fusion.50), channel_id=1, source_target_pairs={{0,4},{2,6},{4,0},{6,2},{1,5},{3,7},{5,1},{7,3},{8,12},{10,14},{12... | collective-permute-start | bytes 393224 | tf_op jit(solution)/shard_map/ppermute | solution.py:37
  613.1 15.0 %collective-permute-start.70 = (f32[128,512]{0,1:T(8,128)S(1)}, f32[128,512]{0,1:T(8,128)S(1)}, u32[]{:S(2)}, u32[]{:S(2)}) collective-permute-start(f32[128,512]{0,1:T(8,128)S(1)} %convert_add_fusion.2), channel_id=1, source_target_pairs={{0,2},{2,0},{4,6},{6,4},{1,3},{3,1},{5,7},{7,5},{8,10},{10,8},{12,... | collective-permute-start | bytes 786440 | tf_op jit(solution)/shard_map/ppermute | solution.py:33
  621.6 73.6 %collective-permute-start.50 = (bf16[8,512,256]{2,1,0:T(8,128)(2,1)S(1)}, bf16[8,512,256]{2,1,0:T(8,128)(2,1)}, u32[]{:S(2)}, u32[]{:S(2)}) collective-permute-start(bf16[8,512,256]{2,1,0:T(8,128)(2,1)S(1)} %add_convert_fusion.1.mine_ref), channel_id=1, source_target_pairs={{0,2},{2,0},{4,6},{6,4},{1,3},{3,1},{5,7},{7,5},{8,10},{10,8},{12,... | collective-permute-start | bytes 6291464 | tf_op jit(solution)/shard_map/ppermute | solution.py:33
  624.1 78.3 %collective-permute-start.48 = (bf16[8,256,512]{2,1,0:T(8,128)(2,1)}, bf16[8,256,512]{2,1,0:T(8,128)(2,1)}, u32[]{:S(2)}, u32[]{:S(2)}) collective-permute-start(bf16[8,256,512]{2,1,0:T(8,128)(2,1)} %add_convert_fusion.2.mine_ref), channel_id=1, source_target_pairs={{0,2},{2,0},{4,6},{6,4},{1,3},{3,1},{5,7},{7,5},{8,10},{10,8},{12,... | collective-permute-start | bytes 6291464 | tf_op jit(solution)/shard_map/ppermute | solution.py:33
  628.1 15.9 %collective-permute-start.43 = (bf16[256,1024]{1,0:T(8,128)(2,1)S(1)}, bf16[256,1024]{1,0:T(8,128)(2,1)S(1)}, u32[]{:S(2)}, u32[]{:S(2)}) collective-permute-start(bf16[256,1024]{1,0:T(8,128)(2,1)S(1)} %get-tuple-element.226), channel_id=1, source_target_pairs={{0,24},{8,0},{16,8},{24,16},{1,25},{9,1},{17,9},{25,17},{2,26},{10... | collective-permute-start | bytes 1572872 | tf_op jit(solution)/shard_map/ppermute | solution.py:41
  644.0 16.7 %collective-permute-start.44 = (bf16[256,1024]{1,0:T(8,128)(2,1)S(1)}, bf16[256,1024]{1,0:T(8,128)(2,1)S(1)}, u32[]{:S(2)}, u32[]{:S(2)}) collective-permute-start(bf16[256,1024]{1,0:T(8,128)(2,1)S(1)} %get-tuple-element.225), channel_id=1, source_target_pairs={{0,8},{8,16},{16,24},{24,0},{1,9},{9,17},{17,25},{25,1},{2,10},{10... | collective-permute-start | bytes 1572872 | tf_op jit(solution)/shard_map/ppermute | solution.py:41
  646.1 35.9 %collective-permute-start.45 = (bf16[256,1024]{1,0:T(8,128)(2,1)S(1)}, bf16[256,1024]{1,0:T(8,128)(2,1)S(1)}, u32[]{:S(2)}, u32[]{:S(2)}) collective-permute-start(bf16[256,1024]{1,0:T(8,128)(2,1)S(1)} %get-tuple-element.224), channel_id=1, source_target_pairs={{0,16},{8,24},{16,0},{24,8},{1,17},{9,25},{17,1},{25,9},{2,18},{10... | collective-permute-start | bytes 1572872 | tf_op jit(solution)/shard_map/ppermute | solution.py:41
  649.2 80.6 %collective-permute-start.84 = (bf16[8,512,256]{2,1,0:T(8,128)(2,1)}, bf16[8,512,256]{2,1,0:T(8,128)(2,1)}, u32[]{:S(2)}, u32[]{:S(2)}) collective-permute-start(bf16[8,512,256]{2,1,0:T(8,128)(2,1)} %add_convert_fusion.mine_ref), channel_id=1, source_target_pairs={{0,2},{2,0},{4,6},{6,4},{1,3},{3,1},{5,7},{7,5},{8,10},{10,8},{12,... | collective-permute-start | bytes 6291464 | tf_op jit(solution)/shard_map/ppermute | solution.py:33
  660.7 30.2 %collective-permute-start.55 = (f32[1,1024]{1,0:T(1,128)S(1)}, f32[1,1024]{1,0:T(1,128)S(1)}, u32[]{:S(2)}, u32[]{:S(2)}) collective-permute-start(f32[1,1024]{1,0:T(1,128)S(1)} %add.565), channel_id=1, source_target_pairs={{0,4},{2,6},{4,0},{6,2},{1,5},{3,7},{5,1},{7,3},{8,12},{10,14},{12... | collective-permute-start | bytes 12296 | tf_op jit(solution)/shard_map/ppermute | solution.py:37
  690.9 20.1 %collective-permute-start.56 = (f32[1,256]{1,0:T(1,128)S(1)}, f32[1,256]{1,0:T(1,128)S(1)}, u32[]{:S(2)}, u32[]{:S(2)}) collective-permute-start(f32[1,256]{1,0:T(1,128)S(1)} %get-tuple-element.273), channel_id=1, source_target_pairs={{0,8},{8,16},{16,24},{24,0},{1,9},{9,17},{17,25},{25,1},{2,10},{10... | collective-permute-start | bytes 3080 | tf_op jit(solution)/shard_map/ppermute | solution.py:41
  691.6 20.8 %collective-permute-start.57 = (f32[1,256]{1,0:T(1,128)S(1)}, f32[1,256]{1,0:T(1,128)S(1)}, u32[]{:S(2)}, u32[]{:S(2)}) collective-permute-start(f32[1,256]{1,0:T(1,128)S(1)} %get-tuple-element.275), channel_id=1, source_target_pairs={{0,16},{8,24},{16,0},{24,8},{1,17},{9,25},{17,1},{25,9},{2,18},{10... | collective-permute-start | bytes 3080 | tf_op jit(solution)/shard_map/ppermute | solution.py:41
  695.3 19.9 %collective-permute-start.58 = (f32[1,256]{1,0:T(1,128)S(1)}, f32[1,256]{1,0:T(1,128)S(1)}, u32[]{:S(2)}, u32[]{:S(2)}) collective-permute-start(f32[1,256]{1,0:T(1,128)S(1)} %get-tuple-element.274), channel_id=1, source_target_pairs={{0,24},{8,0},{16,8},{24,16},{1,25},{9,1},{17,9},{25,17},{2,26},{10... | collective-permute-start | bytes 3080 | tf_op jit(solution)/shard_map/ppermute | solution.py:41
  (132 other events, 2071.3 us)
Sparse Core Ops, SparseCore 0:
  9.6 36.2 all-gather.2
  48.6 84.9 all-gather.4
